TPU v7x, 32 devices: a whole 2x2x4 slice. The times are simulated.
32 devices in a mesh: body: 2 (over core), gx: 4 (over z), gy: 4 (over y, x).
Axes of the slice: x: 2, y: 2, z: 4, core: 2. Of those that a mesh axis runs over, the one named last changes fastest.
Arguments:
- disp: float32 [2, 3, 32, 128, 128], P('body', None, 'gx', 'gy'), may hold values from -4 to 4
- force: float32 [2, 3, 32, 128, 128], P('body', None, 'gx', 'gy'), may hold values from -12 to 12
- kappa: float32 [2, 32, 128, 128], P('body', 'gx', 'gy'), may hold values from 0.05 to 0.5
- sigma: float32 [2, 32, 128, 128], P('body', 'gx', 'gy'), may hold values from 0.2 to 1
- gap0: float32 [32, 128], P(('gx', 'gy')), may hold values from -3 to 3
- pressure: float32 [32, 128], P(('gx', 'gy')), may hold values from 0 to 1
- mortar: float32 [32, 128, 128], P(('gx', 'gy')), may hold values from -0.5 to 0.5
- partner: int32 [32], P(('gx', 'gy')), may hold values from 0 to 7
- active: int32 [32], P(('gx', 'gy')), may hold values 0 or 1
Outputs:
- increment: float32 [2, 3, 32, 128, 128], P('body', None, 'gx', 'gy')
- new_pressure: float32 [32, 128], P(('gx', 'gy'))
Inputs may be any that keep to these rules, and one draw needn't show every extreme that they name: partner numbers a master block of the same gy index: gx index times 2 plus the local block. 1 marks a block of the active contact set.
All inputs are finite; a program needn't handle non-finite values.
Results may differ from a plain program's by a relative error of at most 0.00015.
Values sent between devices are 32-bit elements; how exact they have to be, the bound alone decides.
A program may use at most 64 MiB of HBM per device.

v0:
```python
import jax
import jax.numpy as jnp
from jax import lax
from jax.sharding import PartitionSpec as P

SBLK = 128
CG_ITERS = 2


def extended(block, sides, width):
    for axis, dim in sides:
        count = lax.axis_size(axis)
        forward = [(i, i + 1) for i in range(count - 1)]
        backward = [(target, source) for source, target in forward]
        low = lax.ppermute(
            lax.slice_in_dim(block, block.shape[dim] - width, None, axis=dim), axis, forward
        )
        high = lax.ppermute(lax.slice_in_dim(block, 0, width, axis=dim), axis, backward)
        block = jnp.concatenate([low, block, high], axis=dim)
    return block


def neighbours():
    result = []
    for first in (-1, 0, 1):
        for second in (-1, 0, 1):
            for third in (-1, 0, 1):
                if first != 0 or second != 0 or third != 0:
                    result.append((first, second, third))
    return result


def apply_stencil(field, padded, kappa, kappa_rim, sigma):
    sizes = field.shape[2:]
    total = sigma[:, None] * field
    for offset in neighbours():
        weight = 0.5 ** (abs(offset[0]) + abs(offset[1]) + abs(offset[2]) - 1)
        lower = [1 + offset[0], 1 + offset[1], 1 + offset[2]]
        bond = 0.5 * (
            kappa
            + kappa_rim[
                :,
                lower[0] : lower[0] + sizes[0],
                lower[1] : lower[1] + sizes[1],
                lower[2] : lower[2] + sizes[2],
            ]
        )
        near = padded[
            :,
            :,
            lower[0] : lower[0] + sizes[0],
            lower[1] : lower[1] + sizes[1],
            lower[2] : lower[2] + sizes[2],
        ]
        total = total + weight * bond[:, None] * (field - near)
    return total


def stencil(field, kappa, kappa_rim, sigma):
    padded = extended(field, (("gx", 2), ("gy", 3)), 1)
    padded = jnp.pad(padded, ((0, 0), (0, 0), (0, 0), (0, 0), (1, 1)))
    return apply_stencil(field, padded, kappa, kappa_rim, sigma)


def gap_of(field, selector, mortar):
    own = field[0, 2, :, :, 0].reshape(1, -1, SBLK)
    rows = lax.all_gather(own, ("body", "gx"), axis=0, tiled=True)
    row_count = lax.axis_size("gx")
    slave_own = lax.dynamic_index_in_dim(rows, lax.axis_index("gx"), 0, keepdims=False)
    master_row = rows[row_count:].reshape(-1, SBLK)
    picked = jnp.dot(selector, master_row, precision=lax.Precision.HIGHEST)
    pulled = jnp.einsum("bij,bj->bi", mortar, picked, precision=lax.Precision.HIGHEST)
    return -slave_own - pulled


def spread(traction, selector, mortar):
    pulled = jnp.einsum("bij,bi->bj", mortar, traction, precision=lax.Precision.HIGHEST)
    row_terms = -jnp.dot(selector.T, pulled, precision=lax.Precision.HIGHEST)
    share = lax.psum_scatter(row_terms, "gx", scatter_dimension=0, tiled=True)
    return jnp.where(lax.axis_index("body") == 0, -traction, share)


def add_surface(image, surface):
    return image.at[0, 2, :, :, 0].add(surface.reshape(image.shape[2], image.shape[3]))


def two_products(residual, image):
    return lax.psum((jnp.sum(residual * residual), jnp.sum(residual * image)), ("body", "gx", "gy"))


def on_device(disp, force, kappa, sigma, gap0, pressure, mortar, partner, active):
    kappa_rim = extended(kappa, (("gx", 1), ("gy", 2)), 1)
    kappa_rim = jnp.pad(kappa_rim, ((0, 0), (0, 0), (0, 0), (1, 1)))
    row_blocks = mortar.shape[0] * lax.axis_size("gx")
    selector = (partner[:, None] == jnp.arange(row_blocks, dtype=jnp.int32)[None, :]).astype(
        jnp.float32
    )
    flags = active.astype(jnp.float32)[:, None]
    gap = gap0 + gap_of(disp, selector, mortar)
    radius = jnp.sqrt(gap * gap + pressure * pressure + 0.01)
    complement = gap + pressure - radius
    slope_gap = 1.0 - gap / radius
    slope_press = 1.0 - pressure / radius
    divisor = slope_press + 0.5
    stiffness = flags * slope_gap / divisor
    excess = flags * complement / divisor
    rhs = force - stencil(disp, kappa, kappa_rim, sigma)
    rhs = add_surface(rhs, spread(flags * pressure - excess, selector, mortar))

    def operate(field):
        image = stencil(field, kappa, kappa_rim, sigma)
        return add_surface(
            image, spread(stiffness * gap_of(field, selector, mortar), selector, mortar)
        )

    increment = jnp.zeros_like(rhs)
    residual = rhs
    image = operate(residual)
    norm_now, product = two_products(residual, image)
    alpha = norm_now / product
    direction, along = (residual, image)
    for step in range(CG_ITERS):
        increment = increment + alpha * direction
        residual = residual - alpha * along
        if step + 1 < CG_ITERS:
            image = operate(residual)
            norm_next, product = two_products(residual, image)
            ratio = norm_next / norm_now
            alpha = norm_next / (product - ratio * norm_next / alpha)
            direction = residual + ratio * direction
            along = image + ratio * along
            norm_now = norm_next
    change = gap_of(increment, selector, mortar)
    new_press = flags * (pressure - (complement + slope_gap * change) / divisor)
    return (increment, new_press)


def solution(mesh):
    placed = (
        P("body", None, "gx", "gy", None),
        P("body", None, "gx", "gy", None),
        P("body", "gx", "gy", None),
        P("body", "gx", "gy", None),
        P(("gx", "gy"), None),
        P(("gx", "gy"), None),
        P(("gx", "gy"), None, None),
        P(("gx", "gy")),
        P(("gx", "gy")),
    )
    return jax.shard_map(
        on_device,
        mesh=mesh,
        in_specs=placed,
        out_specs=(P("body", None, "gx", "gy", None), P(("gx", "gy"), None)),
        check_vma=False,
    )
```

profile of v0, /device:TPU:0, one launch (start us, length us, event | category | flops | bytes accessed | tf_op | source)
XLA Modules:
  0.0 263.3 jit_solution(12409039478095892816)
XLA Ops:
  0.7 0.9 fusion.261
  1.5 4.9 %collective-permute-start.4 = (f32[1,3,1,32,128]{4,3,2,1,0:T(8,128)S(1)}, f32[1,3,1,32,128]{4,3,2,1,0:T(8,128)S(1)}, u32[]{:S(2)}, u32[]{:S(2)}) collective-permute-start(f32[1,3,1,32,128]{4,3,2,1,0:T(8,128)S(1)} %get-tuple-element.86), channel_id=1, source_target_pairs={{0,4},{4,8},{8,12},{1,5},{5,9},{9,13},{2,6},{6,10},{10,14},{3,7},{... | collective-permute-start | bytes 147464 | tf_op jit(solution)/shard_map/ppermute | solution.py:15
  6.5 1.3 collective-permute-start.5
  7.8 0.7 fusion.263
  8.5 4.5 %collective-permute-start = (f32[1,1,32,128]{3,2,1,0:T(8,128)S(1)}, f32[1,1,32,128]{3,2,1,0:T(8,128)S(1)}, u32[]{:S(2)}, u32[]{:S(2)}) collective-permute-start(f32[1,1,32,128]{3,2,1,0:T(8,128)S(1)} %get-tuple-element.101), channel_id=1, source_target_pairs={{0,4},{4,8},{8,12},{1,5},{5,9},{9,13},{2,6},{6,10},{10,14},{3,7},{... | collective-permute-start | bytes 49160 | tf_op jit(solution)/shard_map/ppermute | solution.py:15
  13.1 1.3 collective-permute-start.1
  14.4 1.0 slice_reduce_fusion.2
  15.4 0.7 convert_element_type.10
  16.1 15.7 %all_gather.12 = f32[8,2,128]{2,1,0:T(2,128)S(1)} all-gather(f32[1,2,128]{2,1,0:T(2,128)S(1)} %reshape_squeeze.12), channel_id=1, replica_groups=mesh['body'=2,'gx'=4,'gy'=4] {'body','gx'}, dimensions={0}, use_global_device_ids=true | all-gather | bytes 9216 | tf_op jit(solution)/shard_map/all_gather | solution.py:67
  31.9 0.8 fusion.248
  32.7 0.3 fusion.264
  33.0 0.8 divide_subtract_fusion
  33.8 0.2 fusion.265
  34.0 0.9 convolution_negate_fusion.2
  34.9 1.2 dynamic-slice.22
  36.8 10.1 %all-reduce.4 = f32[8,128]{1,0:T(8,128)S(1)} all-reduce(f32[8,128]{1,0:T(8,128)S(1)} %convolution_negate_fusion.2), channel_id=2, replica_groups=mesh['body'=2,'gx'=4,'gy'=4] {'gx'}, use_global_device_ids=true, to_apply=%region_0.1.clone | all-reduce | flops 1024 | bytes 8192
  46.9 0.9 constant_dynamic-update-slice_fusion.1
  47.9 1.3 collective-permute-start.3
  49.2 4.5 %collective-permute-start.2 = (f32[1,10,1,128]{3,2,1,0:T(1,128)S(1)}, f32[1,10,1,128]{3,2,1,0:T(1,128)S(1)}, u32[]{:S(2)}, u32[]{:S(2)}) collective-permute-start(f32[1,10,1,128]{3,2,1,0:T(1,128)S(1)} %get-tuple-element.96), channel_id=1, source_target_pairs={{0,1},{1,2},{2,3},{4,5},{5,6},{6,7},{8,9},{9,10},{10,11},{12,13},{... | collective-permute-start | bytes 15368 | tf_op jit(solution)/shard_map/ppermute | solution.py:15
  54.0 1.1 collective-permute-done.2
  55.1 0.2 select_maximum_fusion.10
  55.3 0.5 fusion.238
  55.8 0.5 copy-done.1
  56.4 1.3 collective-permute-start.7
  57.7 4.9 %collective-permute-start.6 = (f32[1,3,10,1,128]{4,3,2,1,0:T(1,128)S(1)}, f32[1,3,10,1,128]{4,3,2,1,0:T(1,128)S(1)}, u32[]{:S(2)}, u32[]{:S(2)}) collective-permute-start(f32[1,3,10,1,128]{4,3,2,1,0:T(1,128)S(1)} %get-tuple-element.79), channel_id=1, source_target_pairs={{0,1},{1,2},{2,3},{4,5},{5,6},{6,7},{8,9},{9,10},{10,11},{12,13},{... | collective-permute-start | bytes 46088 | tf_op jit(solution)/shard_map/ppermute | solution.py:15
  62.9 1.2 collective-permute-done.6
  64.0 0.5 select_maximum_fusion.8
  64.6 2.4 fusion.16
  67.3 1.3 collective-permute-start.9
  68.6 4.5 %collective-permute-start.8 = (f32[1,3,1,32,128]{4,3,2,1,0:T(8,128)S(1)}, f32[1,3,1,32,128]{4,3,2,1,0:T(8,128)S(1)}, u32[]{:S(2)}, u32[]{:S(2)}) collective-permute-start(f32[1,3,1,32,128]{4,3,2,1,0:T(8,128)S(1)} %get-tuple-element.83), channel_id=1, source_target_pairs={{0,4},{4,8},{8,12},{1,5},{5,9},{9,13},{2,6},{6,10},{10,14},{3,7},{... | collective-permute-start | bytes 147464 | tf_op jit(solution)/shard_map/ppermute | solution.py:15
  73.3 13.0 %all_gather.13 = f32[8,2,128]{2,1,0:T(2,128)S(1)} all-gather(f32[1,2,128]{2,1,0:T(2,128)S(1)} %reshape_squeeze.13), channel_id=1, replica_groups=mesh['body'=2,'gx'=4,'gy'=4] {'body','gx'}, dimensions={0}, use_global_device_ids=true | all-gather | bytes 9216 | tf_op jit(solution)/shard_map/all_gather | solution.py:67
  86.5 0.3 fusion.266
  86.8 0.7 fusion.243
  87.7 0.3 convolution_negate_fusion.1
  87.9 10.4 %all-reduce.5 = f32[8,128]{1,0:T(8,128)S(1)} all-reduce(f32[8,128]{1,0:T(8,128)S(1)} %convolution_negate_fusion.1), channel_id=3, replica_groups=mesh['body'=2,'gx'=4,'gy'=4] {'gx'}, use_global_device_ids=true, to_apply=%region_3.4.clone | all-reduce | flops 1024 | bytes 8192
  98.4 1.3 collective-permute-start.11
  99.7 5.7 %collective-permute-start.10 = (f32[1,3,10,1,128]{4,3,2,1,0:T(1,128)S(1)}, f32[1,3,10,1,128]{4,3,2,1,0:T(1,128)S(1)}, u32[]{:S(2)}, u32[]{:S(2)}) collective-permute-start(f32[1,3,10,1,128]{4,3,2,1,0:T(1,128)S(1)} %get-tuple-element.77), channel_id=1, source_target_pairs={{0,1},{1,2},{2,3},{4,5},{5,6},{6,7},{8,9},{9,10},{10,11},{12,13},{... | collective-permute-start | bytes 46088 | tf_op jit(solution)/shard_map/ppermute | solution.py:15
  105.4 0.9 reshape.409
  106.3 0.5 collective-permute-done.10
  106.8 0.5 select_maximum_fusion.4
  107.6 0.7 copy-done.9
  108.6 2.9 %fusion.95 = f32[1,3,8,32,128]{4,3,2,1,0:T(8,128)S(1)} fusion(f32[1,3,8,32,128]{4,3,2,1,0:T(8,128)S(1)} %scatter-add.10, f32[1,3,10,34,130]{4,3,2,1,0:T(8,128)S(1)} %select_maximum_fusion.4, f32[1,3,10,33,128]{4,3,2,1,0:T(8,128)S(1)} %get-tuple-element.76, f32[1,3,1,32,128]{4,3,2,1,0:T(8,128)} %copy-done.32, ...), kind=kLoop, calls=%fused_computation.153 | loop fusion | flops 7962624 | bytes 13860864 | tf_op jit(solution)/shard_map/add | solution.py:55
  111.7 0.8 multiply_reduce_fusion.2
  112.5 41.8 %all-reduce.8 = (f32[]{:T(128)}, f32[]{:T(128)}) all-reduce(f32[]{:T(128)} %get-tuple-element.41, f32[]{:T(128)} %get-tuple-element.40), channel_id=1, replica_groups=mesh['body'=2,'gx'=4,'gy'=4] {'body','gx','gy'}, use_global_device_ids=true, to_apply=%region_2.3 | all-reduce | flops 2 | bytes 16 | tf_op jit(solution)/shard_map/psum | solution.py:88
  155.8 1.3 collective-permute-start.13
  157.1 4.7 %collective-permute-start.12 = (f32[1,3,1,32,128]{4,3,2,1,0:T(8,128)S(1)}, f32[1,3,1,32,128]{4,3,2,1,0:T(8,128)S(1)}, u32[]{:S(2)}, u32[]{:S(2)}) collective-permute-start(f32[1,3,1,32,128]{4,3,2,1,0:T(8,128)S(1)} %get-tuple-element.81), channel_id=1, source_target_pairs={{0,4},{4,8},{8,12},{1,5},{5,9},{9,13},{2,6},{6,10},{10,14},{3,7},{... | collective-permute-start | bytes 147464 | tf_op jit(solution)/shard_map/ppermute | solution.py:15
  161.9 14.8 %all_gather.14 = f32[8,2,128]{2,1,0:T(2,128)S(1)} all-gather(f32[1,2,128]{2,1,0:T(2,128)S(1)} %reshape_squeeze.14), channel_id=1, replica_groups=mesh['body'=2,'gx'=4,'gy'=4] {'body','gx'}, dimensions={0}, use_global_device_ids=true | all-gather | bytes 9216 | tf_op jit(solution)/shard_map/all_gather | solution.py:67
  176.7 0.8 fusion.246
  177.5 0.3 fusion.268
  177.8 0.7 fusion.242
  178.7 0.9 convolution_negate_fusion
  179.6 9.0 %all-reduce.6 = f32[8,128]{1,0:T(8,128)S(1)} all-reduce(f32[8,128]{1,0:T(8,128)S(1)} %convolution_negate_fusion), channel_id=4, replica_groups=mesh['body'=2,'gx'=4,'gy'=4] {'gx'}, use_global_device_ids=true, to_apply=%region_8.9.clone | all-reduce | flops 1024 | bytes 8192
  188.7 1.3 collective-permute-start.15
  190.0 4.8 %collective-permute-start.14 = (f32[1,3,10,1,128]{4,3,2,1,0:T(1,128)S(1)}, f32[1,3,10,1,128]{4,3,2,1,0:T(1,128)S(1)}, u32[]{:S(2)}, u32[]{:S(2)}) collective-permute-start(f32[1,3,10,1,128]{4,3,2,1,0:T(1,128)S(1)} %get-tuple-element.73), channel_id=1, source_target_pairs={{0,1},{1,2},{2,3},{4,5},{5,6},{6,7},{8,9},{9,10},{10,11},{12,13},{... | collective-permute-start | bytes 46088 | tf_op jit(solution)/shard_map/ppermute | solution.py:15
  194.8 0.9 reshape.410
  195.6 0.5 collective-permute-done.14
  196.2 0.5 select_maximum_fusion
  196.9 0.7 copy-done.3
  198.1 2.9 %fusion.41 = f32[1,3,8,32,128]{4,3,2,1,0:T(8,128)S(1)} fusion(f32[1,3,8,32,128]{4,3,2,1,0:T(8,128)S(1)} %multiply_subtract_fusion, f32[1,3,10,34,130]{4,3,2,1,0:T(8,128)S(1)} %select_maximum_fusion, f32[1,3,10,33,128]{4,3,2,1,0:T(8,128)S(1)} %get-tuple-element.72, f32[1,3,1,32,128]{4,3,2,1,0:T(8,128)} %copy-done.30, ...), kind=kLoop, calls=%fused_computation.73 | loop fusion | flops 7962624 | bytes 13860864 | tf_op jit(solution)/shard_map/add | solution.py:55
  201.2 0.7 multiply_reduce_fusion
  202.0 42.0 %all-reduce.7 = (f32[]{:T(128)}, f32[]{:T(128)}) all-reduce(f32[]{:T(128)} %get-tuple-element.39, f32[]{:T(128)} %get-tuple-element.38), channel_id=1, replica_groups=mesh['body'=2,'gx'=4,'gy'=4] {'body','gx','gy'}, use_global_device_ids=true, to_apply=%region_7.8 | all-reduce | flops 2 | bytes 16 | tf_op jit(solution)/shard_map/psum | solution.py:88
  248.8 13.4 %all_gather.15 = f32[8,2,128]{2,1,0:T(2,128)S(1)} all-gather(f32[1,2,128]{2,1,0:T(2,128)S(1)} %reshape_squeeze.15), channel_id=1, replica_groups=mesh['body'=2,'gx'=4,'gy'=4] {'body','gx'}, dimensions={0}, use_global_device_ids=true | all-gather | bytes 9216 | tf_op jit(solution)/shard_map/all_gather | solution.py:67
  262.4 0.3 fusion.270
  262.7 0.7 subtract_multiply_fusion
  (131 shorter events, 3.8 us)
Async XLA Ops:
  0.6 32.1 %copy-start = (f32[2,128,128]{2,1,0:T(8,128)S(1)}, f32[2,128,128]{2,1,0:T(8,128)}, u32[]{:S(2)}) copy-start(f32[2,128,128]{2,1,0:T(8,128)} %param.21) | copy-start | bytes 393220
  0.6 54.7 %copy-start.26 = (f32[1,8,32,128]{3,2,1,0:T(8,128)S(1)}, f32[1,8,32,128]{3,2,1,0:T(8,128)}, u32[]{:S(2)}) copy-start(f32[1,8,32,128]{3,2,1,0:T(8,128)} %param.17) | copy-start | bytes 393220
  1.5 54.3 %collective-permute-start.4 = (f32[1,3,1,32,128]{4,3,2,1,0:T(8,128)S(1)}, f32[1,3,1,32,128]{4,3,2,1,0:T(8,128)S(1)}, u32[]{:S(2)}, u32[]{:S(2)}) collective-permute-start(f32[1,3,1,32,128]{4,3,2,1,0:T(8,128)S(1)} %get-tuple-element.86), channel_id=1, source_target_pairs={{0,4},{4,8},{8,12},{1,5},{5,9},{9,13},{2,6},{6,10},{10,14},{3,7},{... | collective-permute-start | bytes 147464 | tf_op jit(solution)/shard_map/ppermute | solution.py:15
  6.5 49.9 %collective-permute-start.5 = (f32[1,3,1,32,128]{4,3,2,1,0:T(8,128)S(1)}, f32[1,3,1,32,128]{4,3,2,1,0:T(8,128)S(1)}, u32[]{:S(2)}, u32[]{:S(2)}) collective-permute-start(f32[1,3,1,32,128]{4,3,2,1,0:T(8,128)S(1)} %get-tuple-element.85), channel_id=1, source_target_pairs={{4,0},{8,4},{12,8},{5,1},{9,5},{13,9},{6,2},{10,6},{14,10},{7,3},{... | collective-permute-start | bytes 147464 | tf_op jit(solution)/shard_map/ppermute | solution.py:18
  8.5 38.4 %collective-permute-start = (f32[1,1,32,128]{3,2,1,0:T(8,128)S(1)}, f32[1,1,32,128]{3,2,1,0:T(8,128)S(1)}, u32[]{:S(2)}, u32[]{:S(2)}) collective-permute-start(f32[1,1,32,128]{3,2,1,0:T(8,128)S(1)} %get-tuple-element.101), channel_id=1, source_target_pairs={{0,4},{4,8},{8,12},{1,5},{5,9},{9,13},{2,6},{6,10},{10,14},{3,7},{... | collective-permute-start | bytes 49160 | tf_op jit(solution)/shard_map/ppermute | solution.py:15
  13.1 34.8 %collective-permute-start.1 = (f32[1,1,32,128]{3,2,1,0:T(8,128)S(1)}, f32[1,1,32,128]{3,2,1,0:T(8,128)S(1)}, u32[]{:S(2)}, u32[]{:S(2)}) collective-permute-start(f32[1,1,32,128]{3,2,1,0:T(8,128)S(1)} %get-tuple-element.100), channel_id=1, source_target_pairs={{4,0},{8,4},{12,8},{5,1},{9,5},{13,9},{6,2},{10,6},{14,10},{7,3},{... | collective-permute-start | bytes 49160 | tf_op jit(solution)/shard_map/ppermute | solution.py:18
  47.9 6.1 %collective-permute-start.3 = (f32[1,10,1,128]{3,2,1,0:T(1,128)S(1)}, f32[1,10,1,128]{3,2,1,0:T(1,128)S(1)}, u32[]{:S(2)}, u32[]{:S(2)}) collective-permute-start(f32[1,10,1,128]{3,2,1,0:T(1,128)S(1)} %get-tuple-element.97), channel_id=1, source_target_pairs={{1,0},{2,1},{3,2},{5,4},{6,5},{7,6},{9,8},{10,9},{11,10},{13,12},{... | collective-permute-start | bytes 15368 | tf_op jit(solution)/shard_map/ppermute | solution.py:18
  49.2 5.9 %collective-permute-start.2 = (f32[1,10,1,128]{3,2,1,0:T(1,128)S(1)}, f32[1,10,1,128]{3,2,1,0:T(1,128)S(1)}, u32[]{:S(2)}, u32[]{:S(2)}) collective-permute-start(f32[1,10,1,128]{3,2,1,0:T(1,128)S(1)} %get-tuple-element.96), channel_id=1, source_target_pairs={{0,1},{1,2},{2,3},{4,5},{5,6},{6,7},{8,9},{9,10},{10,11},{12,13},{... | collective-permute-start | bytes 15368 | tf_op jit(solution)/shard_map/ppermute | solution.py:15
  55.3 1.0 copy-start.1
  55.8 51.7 %copy-start.2 = (f32[8,32,128]{2,1,0:T(8,128)}, f32[8,32,128]{2,1,0:T(8,128)S(1)}, u32[]{:S(2)}) copy-start(f32[8,32,128]{2,1,0:T(8,128)S(1)} %get-tuple-element.70) | copy-start | bytes 393220
  56.4 6.5 %collective-permute-start.7 = (f32[1,3,10,1,128]{4,3,2,1,0:T(1,128)S(1)}, f32[1,3,10,1,128]{4,3,2,1,0:T(1,128)S(1)}, u32[]{:S(2)}, u32[]{:S(2)}) collective-permute-start(f32[1,3,10,1,128]{4,3,2,1,0:T(1,128)S(1)} %get-tuple-element.80), channel_id=1, source_target_pairs={{1,0},{2,1},{3,2},{5,4},{6,5},{7,6},{9,8},{10,9},{11,10},{13,12},{... | collective-permute-start | bytes 46088 | tf_op jit(solution)/shard_map/ppermute | solution.py:18
  57.7 6.3 %collective-permute-start.6 = (f32[1,3,10,1,128]{4,3,2,1,0:T(1,128)S(1)}, f32[1,3,10,1,128]{4,3,2,1,0:T(1,128)S(1)}, u32[]{:S(2)}, u32[]{:S(2)}) collective-permute-start(f32[1,3,10,1,128]{4,3,2,1,0:T(1,128)S(1)} %get-tuple-element.79), channel_id=1, source_target_pairs={{0,1},{1,2},{2,3},{4,5},{5,6},{6,7},{8,9},{9,10},{10,11},{12,13},{... | collective-permute-start | bytes 46088 | tf_op jit(solution)/shard_map/ppermute | solution.py:15
  62.8 4.2 %copy-start.8 = (f32[8,32,128]{2,1,0:T(8,128)}, f32[8,32,128]{2,1,0:T(8,128)S(1)}, u32[]{:S(2)}) copy-start(f32[8,32,128]{2,1,0:T(8,128)S(1)} %get-tuple-element.89) | copy-start | bytes 393220
  62.8 4.2 %copy-start.11 = (f32[8,32,128]{2,1,0:T(8,128)}, f32[8,32,128]{2,1,0:T(8,128)S(1)}, u32[]{:S(2)}) copy-start(f32[8,32,128]{2,1,0:T(8,128)S(1)} %get-tuple-element.93) | copy-start | bytes 393220
  62.8 4.2 %copy-start.14 = (f32[8,32,128]{2,1,0:T(8,128)}, f32[8,32,128]{2,1,0:T(8,128)S(1)}, u32[]{:S(2)}) copy-start(f32[8,32,128]{2,1,0:T(8,128)S(1)} %get-tuple-element.94) | copy-start | bytes 393220
  62.8 4.2 %copy-start.17 = (f32[8,32,128]{2,1,0:T(8,128)}, f32[8,32,128]{2,1,0:T(8,128)S(1)}, u32[]{:S(2)}) copy-start(f32[8,32,128]{2,1,0:T(8,128)S(1)} %get-tuple-element.95) | copy-start | bytes 393220
  62.8 4.2 %copy-start.20 = (f32[8,32,128]{2,1,0:T(8,128)}, f32[8,32,128]{2,1,0:T(8,128)S(1)}, u32[]{:S(2)}) copy-start(f32[8,32,128]{2,1,0:T(8,128)S(1)} %get-tuple-element.98) | copy-start | bytes 393220
  62.8 4.2 %copy-start.23 = (f32[8,32,128]{2,1,0:T(8,128)}, f32[8,32,128]{2,1,0:T(8,128)S(1)}, u32[]{:S(2)}) copy-start(f32[8,32,128]{2,1,0:T(8,128)S(1)} %get-tuple-element.99) | copy-start | bytes 393220
  62.8 44.7 %copy-start.4 = (f32[8,32,128]{2,1,0:T(8,128)}, f32[8,32,128]{2,1,0:T(8,128)S(1)}, u32[]{:S(2)}) copy-start(f32[8,32,128]{2,1,0:T(8,128)S(1)} %get-tuple-element.87) | copy-start | bytes 393220
  62.8 44.7 %copy-start.6 = (f32[8,32,128]{2,1,0:T(8,128)}, f32[8,32,128]{2,1,0:T(8,128)S(1)}, u32[]{:S(2)}) copy-start(f32[8,32,128]{2,1,0:T(8,128)S(1)} %get-tuple-element.88) | copy-start | bytes 393220
  62.8 1.7 copy-start.27
  62.9 1.7 copy-start.37
  64.6 21.7 %copy-start.39 = (s32[2]{0:T(128)S(1)}, s32[2]{0:T(128)}, u32[]{:S(2)}) copy-start(s32[2]{0:T(128)} %param.22) | copy-start | bytes 28
  64.6 22.2 %copy-start.38 = (f32[2,128]{1,0:T(2,128)S(1)}, f32[2,128]{1,0:T(2,128)}, u32[]{:S(2)}) copy-start(f32[2,128]{1,0:T(2,128)} %param.20) | copy-start | bytes 3076
  67.3 31.0 %collective-permute-start.9 = (f32[1,3,1,32,128]{4,3,2,1,0:T(8,128)S(1)}, f32[1,3,1,32,128]{4,3,2,1,0:T(8,128)S(1)}, u32[]{:S(2)}, u32[]{:S(2)}) collective-permute-start(f32[1,3,1,32,128]{4,3,2,1,0:T(8,128)S(1)} %get-tuple-element.84), channel_id=1, source_target_pairs={{4,0},{8,4},{12,8},{5,1},{9,5},{13,9},{6,2},{10,6},{14,10},{7,3},{... | collective-permute-start | bytes 147464 | tf_op jit(solution)/shard_map/ppermute | solution.py:18
  68.6 29.7 %collective-permute-start.8 = (f32[1,3,1,32,128]{4,3,2,1,0:T(8,128)S(1)}, f32[1,3,1,32,128]{4,3,2,1,0:T(8,128)S(1)}, u32[]{:S(2)}, u32[]{:S(2)}) collective-permute-start(f32[1,3,1,32,128]{4,3,2,1,0:T(8,128)S(1)} %get-tuple-element.83), channel_id=1, source_target_pairs={{0,4},{4,8},{8,12},{1,5},{5,9},{9,13},{2,6},{6,10},{10,14},{3,7},{... | collective-permute-start | bytes 147464 | tf_op jit(solution)/shard_map/ppermute | solution.py:15
  98.3 9.2 %copy-start.32 = (f32[1,3,1,32,128]{4,3,2,1,0:T(8,128)}, f32[1,3,1,32,128]{4,3,2,1,0:T(8,128)S(1)}, u32[]{:S(2)}) copy-start(f32[1,3,1,32,128]{4,3,2,1,0:T(8,128)S(1)} %collective-permute-done.9) | copy-start | bytes 147460
  98.3 9.2 %copy-start.33 = (f32[1,3,1,32,128]{4,3,2,1,0:T(8,128)}, f32[1,3,1,32,128]{4,3,2,1,0:T(8,128)S(1)}, u32[]{:S(2)}) copy-start(f32[1,3,1,32,128]{4,3,2,1,0:T(8,128)S(1)} %collective-permute-done.8) | copy-start | bytes 147460
  98.4 7.9 %collective-permute-start.11 = (f32[1,3,10,1,128]{4,3,2,1,0:T(1,128)S(1)}, f32[1,3,10,1,128]{4,3,2,1,0:T(1,128)S(1)}, u32[]{:S(2)}, u32[]{:S(2)}) collective-permute-start(f32[1,3,10,1,128]{4,3,2,1,0:T(1,128)S(1)} %get-tuple-element.78), channel_id=1, source_target_pairs={{1,0},{2,1},{3,2},{5,4},{6,5},{7,6},{9,8},{10,9},{11,10},{13,12},{... | collective-permute-start | bytes 46088 | tf_op jit(solution)/shard_map/ppermute | solution.py:18
  99.7 7.1 %collective-permute-start.10 = (f32[1,3,10,1,128]{4,3,2,1,0:T(1,128)S(1)}, f32[1,3,10,1,128]{4,3,2,1,0:T(1,128)S(1)}, u32[]{:S(2)}, u32[]{:S(2)}) collective-permute-start(f32[1,3,10,1,128]{4,3,2,1,0:T(1,128)S(1)} %get-tuple-element.77), channel_id=1, source_target_pairs={{0,1},{1,2},{2,3},{4,5},{5,6},{6,7},{8,9},{9,10},{10,11},{12,13},{... | collective-permute-start | bytes 46088 | tf_op jit(solution)/shard_map/ppermute | solution.py:15
  107.3 0.9 copy-start.9
  107.4 1.0 copy-start.12
  107.4 1.0 copy-start.15
  107.4 1.1 copy-start.18
  107.4 1.1 copy-start.21
  107.4 1.2 copy-start.24
  107.4 1.2 copy-start.28
  108.6 2.9 %copy-start.36 = (f32[1,1,8,32,1]{4,3,2,1,0:T(8,128)S(1)}, f32[1,1,8,32,1]{4,3,2,1,0:T(8,128)}, u32[]{:S(2)}) copy-start(f32[1,1,8,32,1]{4,3,2,1,0:T(8,128)} %reshape.409) | copy-start | bytes 3076
  155.8 32.8 %collective-permute-start.13 = (f32[1,3,1,32,128]{4,3,2,1,0:T(8,128)S(1)}, f32[1,3,1,32,128]{4,3,2,1,0:T(8,128)S(1)}, u32[]{:S(2)}, u32[]{:S(2)}) collective-permute-start(f32[1,3,1,32,128]{4,3,2,1,0:T(8,128)S(1)} %get-tuple-element.82), channel_id=1, source_target_pairs={{4,0},{8,4},{12,8},{5,1},{9,5},{13,9},{6,2},{10,6},{14,10},{7,3},{... | collective-permute-start | bytes 147464 | tf_op jit(solution)/shard_map/ppermute | solution.py:18
  157.1 31.5 %collective-permute-start.12 = (f32[1,3,1,32,128]{4,3,2,1,0:T(8,128)S(1)}, f32[1,3,1,32,128]{4,3,2,1,0:T(8,128)S(1)}, u32[]{:S(2)}, u32[]{:S(2)}) collective-permute-start(f32[1,3,1,32,128]{4,3,2,1,0:T(8,128)S(1)} %get-tuple-element.81), channel_id=1, source_target_pairs={{0,4},{4,8},{8,12},{1,5},{5,9},{9,13},{2,6},{6,10},{10,14},{3,7},{... | collective-permute-start | bytes 147464 | tf_op jit(solution)/shard_map/ppermute | solution.py:15
  188.6 8.3 %copy-start.30 = (f32[1,3,1,32,128]{4,3,2,1,0:T(8,128)}, f32[1,3,1,32,128]{4,3,2,1,0:T(8,128)S(1)}, u32[]{:S(2)}) copy-start(f32[1,3,1,32,128]{4,3,2,1,0:T(8,128)S(1)} %collective-permute-done.13) | copy-start | bytes 147460
  188.6 8.3 %copy-start.31 = (f32[1,3,1,32,128]{4,3,2,1,0:T(8,128)}, f32[1,3,1,32,128]{4,3,2,1,0:T(8,128)S(1)}, u32[]{:S(2)}) copy-start(f32[1,3,1,32,128]{4,3,2,1,0:T(8,128)S(1)} %collective-permute-done.12) | copy-start | bytes 147460
  188.7 7.0 %collective-permute-start.15 = (f32[1,3,10,1,128]{4,3,2,1,0:T(1,128)S(1)}, f32[1,3,10,1,128]{4,3,2,1,0:T(1,128)S(1)}, u32[]{:S(2)}, u32[]{:S(2)}) collective-permute-start(f32[1,3,10,1,128]{4,3,2,1,0:T(1,128)S(1)} %get-tuple-element.74), channel_id=1, source_target_pairs={{1,0},{2,1},{3,2},{5,4},{6,5},{7,6},{9,8},{10,9},{11,10},{13,12},{... | collective-permute-start | bytes 46088 | tf_op jit(solution)/shard_map/ppermute | solution.py:18
  190.0 6.2 %collective-permute-start.14 = (f32[1,3,10,1,128]{4,3,2,1,0:T(1,128)S(1)}, f32[1,3,10,1,128]{4,3,2,1,0:T(1,128)S(1)}, u32[]{:S(2)}, u32[]{:S(2)}) collective-permute-start(f32[1,3,10,1,128]{4,3,2,1,0:T(1,128)S(1)} %get-tuple-element.73), channel_id=1, source_target_pairs={{0,1},{1,2},{2,3},{4,5},{5,6},{6,7},{8,9},{9,10},{10,11},{12,13},{... | collective-permute-start | bytes 46088 | tf_op jit(solution)/shard_map/ppermute | solution.py:15
  196.7 0.9 copy-start.3
  196.7 1.0 copy-start.5
  196.7 1.0 copy-start.7
  196.7 1.1 copy-start.10
  196.8 1.1 copy-start.13
  196.8 1.2 copy-start.16
  196.8 1.2 copy-start.19
  196.8 1.2 copy-start.22
  196.8 1.3 copy-start.25
  196.8 1.3 copy-start.29
  198.1 2.9 %copy-start.35 = (f32[1,1,8,32,1]{4,3,2,1,0:T(8,128)S(1)}, f32[1,1,8,32,1]{4,3,2,1,0:T(8,128)}, u32[]{:S(2)}) copy-start(f32[1,1,8,32,1]{4,3,2,1,0:T(8,128)} %reshape.410) | copy-start | bytes 3076
  201.1 61.1 %copy-start.40 = (s32[2]{0:T(128)S(1)}, s32[2]{0:T(128)}, u32[]{:S(2)}) copy-start(s32[2]{0:T(128)} %param.22) | copy-start | bytes 28
  248.6 14.7 %copy-start.34 = (f32[1,3,8,32,128]{4,3,2,1,0:T(8,128)}, f32[1,3,8,32,128]{4,3,2,1,0:T(8,128)S(1)}, u32[]{:S(2)}) copy-start(f32[1,3,8,32,128]{4,3,2,1,0:T(8,128)S(1)} %multiply_add_fusion) | copy-start | bytes 1179652
where the time goes:
time: 266 us; the launch traced here: 263 us
  blocking collectives  170 us (64%)
  starting transfers between devices  49 us (18%)
  other arithmetic  16.1 us (6%)
  local copies, waits for them, and re-layouts  10.6 us (4%)
  between operations  8.07 us (3%)
  matrix products  6.01 us (2%)
  waiting for transfers between devices  3.36 us (1%)
    psum x2, blocking collectives, two_products(): lax.psum((jnp.sum(residual * residual), jnp.sum(residual * image)), ('bod...  83.8 us
    all_gather x4, blocking collectives, gap_of(): rows = lax.all_gather(own, ('body', 'gx'), axis=0, tiled=True)  56.9 us
    ppermute x8, starting transfers between devices, extended(): lax.ppermute(lax.slice_in_dim(block, block.shape[dim] - width, None, axis...  38.7 us
    unnamed x3, blocking collectives  29.5 us
    ppermute x8, starting transfers between devices, extended(): lax.ppermute(lax.slice_in_dim(block, 0, width, axis=dim), axis, backward)  10.3 us
    add x2, other arithmetic, apply_stencil(): total = total + weight * bond[:, None] * (field - near)  5.84 us
  transfers between devices with their start and end apart: 16, of which 4 were waited for; matrix products, arithmetic and copies ran while one was open for 6% of the time, Pallas kernels for 0%

commit v1 on v0

v1 whole, which is shorter than its diff:
```python
import functools

import jax
import jax.numpy as jnp
from jax import lax
from jax.experimental import pallas as pl
from jax.experimental.pallas import tpu as pltpu
from jax.sharding import PartitionSpec as P

MESH = pl.DeviceIdType.MESH
YB = 8
DIRS = tuple((dx, dy) for dx in (-1, 0, 1) for dy in (-1, 0, 1) if dx != 0 or dy != 0)


def kernel(nb, ngx, ngy, disp, force, kappa, sigma, gap0, press, mortar, partner, active,
           inc_out, np_out, f0, f1, f2, v2, diag, force_v, sigma_v, mort, surf, usend, urecv,
           gsend, grecv, cols, load_sem, hs, hr, ss, sr, us, ur, gs, gr):
    comp, cx, cy, nz = force_v.shape
    bpd, sblk = gap0.shape
    per = sblk // cy
    b = lax.axis_index("body")
    gx = lax.axis_index("gx")
    gy = lax.axis_index("gy")

    loads = [
        pltpu.make_async_copy(disp.at[0], f0.at[pl.ds(0, comp), pl.ds(1, cx), pl.ds(YB, cy)], load_sem.at[0]),
        pltpu.make_async_copy(kappa.at[0], f0.at[comp, pl.ds(1, cx), pl.ds(YB, cy)], load_sem.at[1]),
        pltpu.make_async_copy(mortar, mort, load_sem.at[2]),
        pltpu.make_async_copy(sigma.at[0], sigma_v, load_sem.at[3]),
        pltpu.make_async_copy(force.at[0], force_v, load_sem.at[4]),
    ]
    for load in loads:
        load.start()

    def exists(dx, dy):
        good = jnp.bool_(True)
        if dx < 0:
            good = good & (gx >= 1)
        if dx > 0:
            good = good & (gx < ngx - 1)
        if dy < 0:
            good = good & (gy >= 1)
        if dy > 0:
            good = good & (gy < ngy - 1)
        return good

    for f in (f0, f1, f2):
        for c in range(f.shape[0]):
            for x in (0, cx + 1):
                f[c, x] = jnp.zeros(f.shape[2:], f.dtype)
            for x in range(1, cx + 1):
                f[c, x, YB - 1 : YB] = jnp.zeros((1, nz), f.dtype)
                f[c, x, YB + cy : YB + cy + 1] = jnp.zeros((1, nz), f.dtype)

    row_peers = [(db, k) for db in range(nb) for k in range(ngx) if db or k]
    barrier = pltpu.get_barrier_semaphore()
    for db, k in row_peers:
        pl.semaphore_signal(barrier, inc=1, device_id={"body": lax.rem(b + db, nb), "gx": lax.rem(gx + k, ngx)},
                            device_id_type=MESH)
    for k in range(1, ngy):
        pl.semaphore_signal(barrier, inc=1, device_id={"gy": lax.rem(gy + k, ngy)}, device_id_type=MESH)
    expect = len(row_peers) + ngy - 1
    for dx, dy in DIRS:
        if dx and dy:
            here = exists(dx, dy)
            expect = expect + here.astype(jnp.int32)

            @pl.when(here)
            def _():
                pl.semaphore_signal(barrier, inc=1, device_id={"gx": gx + dx, "gy": gy + dy}, device_id_type=MESH)

    lane = lax.broadcasted_iota(jnp.int32, (sblk, nz), 1)
    eye = lax.broadcasted_iota(jnp.int32, (sblk, nz), 0) == lane
    first_lane = lane == 0
    lane_row = lax.broadcasted_iota(jnp.int32, (cy, nz), 1)
    left_w = jnp.where(lane_row == 0, 0.0, 0.5)
    right_w = jnp.where(lane_row == nz - 1, 0.0, 0.5)

    def to_col(row):
        return jnp.sum(jnp.where(eye, row, 0.0), axis=1, keepdims=True)

    def to_row(col):
        return jnp.sum(jnp.where(eye, col, 0.0), axis=0, keepdims=True)

    def tz(v):
        return v + left_w * pltpu.roll(v, 1, 1) + right_w * pltpu.roll(v, nz - 1, 1)

    def surface_rows(f, r):
        for l in range(bpd):
            block = f[comp - 1, 1 + l * per : 1 + (l + 1) * per, YB : YB + cy, :].reshape(sblk, nz)
            surf[r, b, gx, l : l + 1, :] = to_row(block[:, 0:1])

    pending = []

    def halo_copy(f, r, d, dx, dy, sending):
        def part(delta, size, base):
            if delta == 0:
                return pl.ds(base, size), pl.ds(base, size)
            if delta < 0:
                return pl.ds(base, 1), pl.ds(base + size, 1)
            return pl.ds(base + size - 1, 1), pl.ds(base - 1, 1)
        sx, tx = part(dx, cx, 1)
        sy, ty = part(dy, cy, YB)
        allc = pl.ds(0, f.shape[0])
        return pltpu.make_async_remote_copy(
            src_ref=f.at[allc, sx, sy], dst_ref=f.at[allc, tx, ty], send_sem=hs.at[r, d], recv_sem=hr.at[r, d],
            device_id={"gx": gx + dx, "gy": gy + dy}, device_id_type=MESH)

    def halo_send(f, r):
        for d, (dx, dy) in enumerate(DIRS):
            @pl.when(exists(dx, dy))
            def _():
                halo_copy(f, r, d, dx, dy, True).start()

    def halo_wait(f, r):
        for d, (dx, dy) in enumerate(DIRS):
            @pl.when(exists(-dx, -dy))
            def _():
                halo_copy(f, r, d, dx, dy, False).wait_recv()

    def halo_done(f, r):
        for d, (dx, dy) in enumerate(DIRS):
            @pl.when(exists(dx, dy))
            def _():
                halo_copy(f, r, d, dx, dy, True).wait_send()

    def surf_copy(r, i, db, k, incoming):
        ob, og = lax.rem(b + db, nb), lax.rem(gx + k, ngx)
        wb, wg = (ob, og) if incoming else (b, gx)
        return pltpu.make_async_remote_copy(
            src_ref=surf.at[r, wb, wg], dst_ref=surf.at[r, wb, wg], send_sem=ss.at[r, i],
            recv_sem=sr.at[r, wb * ngx + wg], device_id={"body": ob, "gx": og}, device_id_type=MESH)

    def surf_send(r):
        for i, (db, k) in enumerate(row_peers):
            surf_copy(r, i, db, k, False).start()

    def surf_wait(r):
        for i, (db, k) in enumerate(row_peers):
            surf_copy(r, i, db, k, True).wait_recv()

    def u_copy(r, k, incoming):
        og = lax.rem(gx + k, ngx)
        return pltpu.make_async_remote_copy(
            src_ref=usend.at[r, og], dst_ref=urecv.at[r, og if incoming else gx], send_sem=us.at[r, k],
            recv_sem=ur.at[r, og if incoming else gx], device_id={"gx": og}, device_id_type=MESH)

    def g_copy(s, k, incoming):
        og = lax.rem(gy + k, ngy)
        w = og if incoming else gy
        return pltpu.make_async_remote_copy(
            src_ref=grecv.at[s, w], dst_ref=grecv.at[s, w], send_sem=gs.at[s, k], recv_sem=gr.at[s, w],
            device_id={"gy": og}, device_id_type=MESH)

    def g_send(s, r):
        total = surf[r, 0, 0]
        for w in range(1, nb * ngx):
            total = total + surf[r, w // ngx, w % ngx]
        grecv[s, gy] = total
        for k in range(1, ngy):
            g_copy(s, k, False).start()

    def g_take(s):
        for k in range(1, ngy):
            g_copy(s, k, True).wait_recv()
        total = grecv[s, 0]
        for w in range(1, ngy):
            total = total + grecv[s, w]
        norm = jnp.sum(total[bpd : bpd + 1, :], axis=1, keepdims=True)
        product = jnp.sum(total[bpd + 1 : bpd + 2, :], axis=1, keepdims=True)
        return norm, product

    def b_of(r, l):
        picked = jnp.zeros((1, sblk), jnp.float32)
        for g in range(ngx):
            for q in range(bpd):
                picked = picked + jnp.where(partner[l] == g * bpd + q, surf[r, 1, g, q : q + 1, :], 0.0)
        slave = surf[r, 0, gx, l : l + 1, :]
        return -jnp.sum(mort[l] * picked + jnp.where(eye, slave, 0.0), axis=1, keepdims=True)

    def u_start(r):
        pulled = [jnp.sum(mort[l] * cols[5, l], axis=0, keepdims=True) for l in range(bpd)]
        for g in range(ngx):
            for q in range(bpd):
                row = jnp.zeros((1, sblk), jnp.float32)
                for l in range(bpd):
                    row = row + jnp.where(partner[l] == g * bpd + q, pulled[l], 0.0)
                usend[r, g, q : q + 1, :] = row

        @pl.when(b == 1)
        def _():
            for k in range(1, ngx):
                u_copy(r, k, False).start()

    def u_finish(r, f, x0, y0):
        def add(l, col):
            xs = slice(x0 + l * per, x0 + (l + 1) * per)
            block = f[comp - 1, xs, y0 : y0 + cy, :].reshape(sblk, nz)
            f[comp - 1, xs, y0 : y0 + cy, :] = (block - jnp.where(first_lane, col, 0.0)).reshape(per, cy, nz)

        @pl.when(b == 0)
        def _():
            for l in range(bpd):
                add(l, cols[5, l])

        @pl.when(b == 1)
        def _():
            for k in range(1, ngx):
                u_copy(r, k, True).wait_recv()
            urecv[r, gx] = usend[r, gx]
            for l in range(bpd):
                row = urecv[r, 0, l : l + 1, :]
                for g in range(1, ngx):
                    row = row + urecv[r, g, l : l + 1, :]
                add(l, to_col(row))

    def apply(f, emit):
        @pl.loop(0, comp)
        def _(c):
            window = []
            for x in range(cx + 2):
                kap = [f0[comp, x, YB + s : YB + s + cy, :] for s in (-1, 0, 1)]
                val = [f[c, x, YB + s : YB + s + cy, :] for s in (-1, 0, 1)]
                window.append((val[1] + 0.5 * (val[0] + val[2]),
                               kap[1] * val[1] + 0.5 * (kap[0] * val[0] + kap[2] * val[2])))
                if x >= 2:
                    p = window[x - 1][0] + 0.5 * (window[x - 2][0] + window[x][0])
                    q = window[x - 1][1] + 0.5 * (window[x - 2][1] + window[x][1])
                    k0 = f0[comp, x - 1, YB : YB + cy, :]
                    v0 = f[c, x - 1, YB : YB + cy, :]
                    emit(c, x - 2, diag[x - 2] * v0 - k0 * tz(p) - tz(q))

    loads[0].wait()
    loads[1].wait()
    surf[0, b, gx] = jnp.zeros(surf.shape[3:], jnp.float32)
    surface_rows(f0, 0)
    usend[...] = jnp.zeros(usend.shape, jnp.float32)
    pl.semaphore_wait(barrier, expect)

    surf_send(0)
    halo_send(f0, 0)
    for load in loads[2:]:
        load.wait()
    surf_wait(0)
    for l in range(bpd):
        gap = to_col(gap0[l : l + 1, :]) + b_of(0, l)
        prs = to_col(press[l : l + 1, :])
        radius = jnp.sqrt(gap * gap + prs * prs + 0.01)
        complement = gap + prs - radius
        slope_gap = 1.0 - gap / radius
        divisor = (1.0 - prs / radius) + 0.5
        flag = active[l].astype(jnp.float32)
        cols[0, l] = flag * slope_gap / divisor
        cols[1, l] = complement / divisor
        cols[2, l] = slope_gap / divisor
        cols[5, l] = flag * prs - flag * complement / divisor
    u_start(0)
    halo_wait(f0, 0)
    window = []
    for x in range(cx + 2):
        kap = [f0[comp, x, YB + s : YB + s + cy, :] for s in (-1, 0, 1)]
        window.append(kap[1] + 0.5 * (kap[0] + kap[2]))
        if x >= 2:
            p = window[x - 1] + 0.5 * (window[x - 2] + window[x])
            diag[x - 2] = sigma_v[x - 2] + 8.0 * f0[comp, x - 1, YB : YB + cy, :] + tz(p)

    def emit_rhs(c, x, val):
        f1[c, 1 + x, YB : YB + cy, :] = force_v[c, x] - val

    apply(f0, emit_rhs)
    u_finish(0, f1, 1, YB)

    surf[1, b, gx] = jnp.zeros(surf.shape[3:], jnp.float32)
    surface_rows(f1, 1)
    surf_send(1)
    halo_send(f1, 1)
    surf_wait(1)
    for l in range(bpd):
        gap = b_of(1, l)
        cols[3, l] = gap
        cols[5, l] = cols[0, l] * gap
    u_start(1)
    halo_wait(f1, 1)

    def emit_v1(c, x, val):
        f2[c, 1 + x, YB : YB + cy, :] = val

    apply(f1, emit_v1)
    u_finish(1, f2, 1, YB)

    def sums(left, right):
        norm = jnp.zeros((cy, nz), jnp.float32)
        product = jnp.zeros((cy, nz), jnp.float32)
        for c in range(comp):
            for x in range(cx):
                a, m = left(c, x), right(c, x)
                norm = norm + a * a
                product = product + a * m
        return jnp.sum(norm, axis=0, keepdims=True), jnp.sum(product, axis=0, keepdims=True)

    def r0_of(c, x):
        return f1[c, 1 + x, YB : YB + cy, :]

    def v1_of(c, x):
        return f2[c, 1 + x, YB : YB + cy, :]

    surf[2, b, gx] = jnp.zeros(surf.shape[3:], jnp.float32)
    norm, product = sums(r0_of, v1_of)
    surf[2, b, gx, bpd : bpd + 1, :] = norm
    surf[2, b, gx, bpd + 1 : bpd + 2, :] = product
    surface_rows(f2, 2)
    surf_send(2)
    halo_send(f2, 2)
    surf_wait(2)
    g_send(0, 2)
    for l in range(bpd):
        gap = b_of(2, l)
        cols[4, l] = gap
        cols[5, l] = cols[0, l] * gap
    u_start(2)
    halo_wait(f2, 2)

    def emit_v2(c, x, val):
        v2[c, x] = val

    apply(f2, emit_v2)
    u_finish(2, v2, 0, 0)
    norm0, product0 = g_take(0)
    alpha0 = norm0 / product0

    norm, product = sums(lambda c, x: r0_of(c, x) - alpha0 * v1_of(c, x),
                         lambda c, x: v1_of(c, x) - alpha0 * v2[c, x])
    surf[3, b, gx] = jnp.zeros(surf.shape[3:], jnp.float32)
    surf[3, b, gx, bpd : bpd + 1, :] = norm
    surf[3, b, gx, bpd + 1 : bpd + 2, :] = product
    surf_send(3)
    surf_wait(3)
    g_send(1, 3)
    norm1, product1 = g_take(1)
    ratio = norm1 / norm0
    alpha1 = norm1 / (product1 - ratio * norm1 / alpha0)
    coef_r = alpha0 + alpha1 * (1.0 + ratio)
    coef_v = -alpha1 * alpha0
    for c in range(comp):
        for x in range(cx):
            inc_out[0, c, x] = coef_r * r0_of(c, x) + coef_v * v1_of(c, x)
    for l in range(bpd):
        change = coef_r * cols[3, l] + coef_v * cols[4, l]
        flag = active[l].astype(jnp.float32)
        step = to_row(cols[1, l] + cols[2, l] * change)
        np_out[l : l + 1, :] = flag * (press[l : l + 1, :] - step)

    for r, f in enumerate((f0, f1, f2)):
        halo_done(f, r)
    for r in range(4):
        for i, (db, k) in enumerate(row_peers):
            surf_copy(r, i, db, k, False).wait_send()
    for s in range(2):
        for k in range(1, ngy):
            g_copy(s, k, False).wait_send()

    @pl.when(b == 1)
    def _():
        for r in range(3):
            for k in range(1, ngx):
                u_copy(r, k, False).wait_send()


def on_device(disp, force, kappa, sigma, gap0, pressure, mortar, partner, active):
    nb, ngx, ngy = (lax.axis_size(a) for a in ("body", "gx", "gy"))
    _, comp, cx, cy, nz = disp.shape
    bpd, sblk, _ = mortar.shape
    f32 = jnp.float32
    any_spec = pl.BlockSpec(memory_space=pl.ANY)
    vmem = pl.BlockSpec(memory_space=pltpu.VMEM)
    smem = pl.BlockSpec(memory_space=pltpu.SMEM)
    rows = cy + 2 * YB
    dma = pltpu.SemaphoreType.DMA
    return pl.pallas_call(
        functools.partial(kernel, nb, ngx, ngy),
        out_shape=(jax.ShapeDtypeStruct(disp.shape, f32), jax.ShapeDtypeStruct(gap0.shape, f32)),
        in_specs=[any_spec, any_spec, any_spec, any_spec, vmem, vmem, any_spec, smem, smem],
        out_specs=(vmem, vmem),
        scratch_shapes=[
            pltpu.VMEM((comp + 1, cx + 2, rows, nz), f32),
            pltpu.VMEM((comp, cx + 2, rows, nz), f32),
            pltpu.VMEM((comp, cx + 2, rows, nz), f32),
            pltpu.VMEM((comp, cx, cy, nz), f32),
            pltpu.VMEM((cx, cy, nz), f32),
            pltpu.VMEM((comp, cx, cy, nz), f32),
            pltpu.VMEM((cx, cy, nz), f32),
            pltpu.VMEM((bpd, sblk, sblk), f32),
            pltpu.VMEM((4, nb, ngx, 8, sblk), f32),
            pltpu.VMEM((3, ngx, 8, sblk), f32),
            pltpu.VMEM((3, ngx, 8, sblk), f32),
            pltpu.VMEM((8, sblk), f32),
            pltpu.VMEM((2, ngy, 8, sblk), f32),
            pltpu.VMEM((6, bpd, sblk, 1), f32),
            dma((5,)),
            dma((3, len(DIRS))), dma((3, len(DIRS))),
            dma((4, nb * ngx)), dma((4, nb * ngx)),
            dma((3, ngx)), dma((3, ngx)),
            dma((2, ngy)), dma((2, ngy)),
        ],
        compiler_params=pltpu.CompilerParams(collective_id=0, has_side_effects=True,
                                             vmem_limit_bytes=60 * 1024 * 1024),
        name="newton_step",
    )(disp, force, kappa, sigma, gap0, pressure, mortar, partner, active)


def solution(mesh):
    placed = (
        P("body", None, "gx", "gy", None),
        P("body", None, "gx", "gy", None),
        P("body", "gx", "gy", None),
        P("body", "gx", "gy", None),
        P(("gx", "gy"), None),
        P(("gx", "gy"), None),
        P(("gx", "gy"), None, None),
        P(("gx", "gy")),
        P(("gx", "gy")),
    )
    return jax.shard_map(
        on_device,
        mesh=mesh,
        in_specs=placed,
        out_specs=(P("body", None, "gx", "gy", None), P(("gx", "gy"), None)),
        check_vma=False,
    )
```

time: 266 us -> 37.6 us (0.14)
  blocking collectives: 170 us -> 0 us
  starting transfers between devices: 49 us -> 0 us
  Pallas kernels: 0 us -> 34.5 us
  other arithmetic: 16.1 us -> 0 us
  local copies, waits for them, and re-layouts: 10.6 us -> 2.33 us
  between operations: 8.07 us -> 0.65 us
  matrix products: 6.01 us -> 0 us
  waiting for transfers between devices: 3.36 us -> 0 us
    psum x2 -> x0, blocking collectives: 83.8 us -> none  [two_products(): lax.psum((jnp.sum(residual * residual), jnp.sum(residual * image)), ('bod...]
    all_gather x4 -> x0, blocking collectives: 56.9 us -> none  [gap_of(): rows = lax.all_gather(own, ('body', 'gx'), axis=0, tiled=True)]
    ppermute x16 -> x0, starting transfers between devices: 49 us -> none  [the longest x8 38.7 us: extended(): lax.ppermute(lax.slice_in_dim(block, block.shape[dim] - width, None, axis...]
    pallas_call x0 -> x1, Pallas kernels: none -> 34.5 us  [on_device(): pl.pallas_call(functools.partial(kernel, nb, ngx, ngy), out_shape=(jax.Sh...]
    unnamed x3 -> x0, blocking collectives: 29.5 us -> none
    add x6 -> x0, other arithmetic: 6.07 us -> none  [the longest x2 5.84 us: apply_stencil(): total = total + weight * bond[:, None] * (field - near)]
    dot_general x14 -> x0, matrix products: 6.01 us -> none  [the longest x3 2.09 us: spread(): row_terms = -jnp.dot(selector.T, pulled, precision=lax.Precision.HIGHEST)]
    ppermute x16 -> x0, waiting for transfers between devices: 3.36 us -> none  [the longest x8 3.34 us: extended(): lax.ppermute(lax.slice_in_dim(block, block.shape[dim] - width, None, axis...]
  transfers between devices with their start and end apart: 16 -> 0, of which waited for: 4 -> 0; matrix products, arithmetic and copies ran while one was open for 6% -> 0% of each run, Pallas kernels for 0% -> 0%
where the time goes in v1:
time: 37.6 us; the launch traced here: 37.5 us
  Pallas kernels  34.5 us (92%)
  local copies, waits for them, and re-layouts  2.33 us (6%)
  between operations  0.65 us (2%)
    pallas_call x1, Pallas kernels, on_device(): pl.pallas_call(functools.partial(kernel, nb, ngx, ngy), out_shape=(jax.Sh...  34.5 us
    unnamed x4, local copies, waits for them, and re-layouts  2.33 us

profile of v1, /device:TPU:0, one launch (start us, length us, event | category | flops | bytes accessed | tf_op | source)
XLA Modules:
  0.0 37.5 jit_solution(14631093725622039555)
XLA Ops:
  0.6 34.5 %newton_step.1 = (f32[1,3,8,32,128]{4,3,2,1,0:T(8,128)}, f32[2,128]{1,0:T(2,128)}) custom-call(f32[1,3,8,32,128]{4,3,2,1,0:T(8,128)} %disp.1, f32[1,3,8,32,128]{4,3,2,1,0:T(8,128)} %force.1, f32[1,8,32,128]{3,2,1,0:T(8,128)} %kappa.1, f32[1,8,32,128]{3,2,1,0:T(8,128)} %sigma.1, f32[2,128]{1,0:T(2,128)} %gap0.1, f32[2,128]{1,0:T(2,128)} %press.1, ...), custom_call_target="tpu_custom_call" | custom-call | tf_op jit(solution)/shard_map/newton_step/pallas_call | solution.py:379
  35.1 0.0 copy-start
  35.1 1.8 %copy.13 = f32[1,3,8,32,128]{4,3,2,1,0:T(8,128)} copy(f32[1,3,8,32,128]{4,3,2,1,0:T(8,128)} %get-tuple-element.4) | data formatting | bytes 786432
  36.9 0.0 copy-done
  36.9 0.6 %copy.14 = f32[2,128]{1,0:T(2,128)} copy(f32[2,128]{1,0:T(2,128)S(1)} %copy-done) | data formatting | bytes 2048
Async XLA Ops:
  35.1 1.8 %copy-start = (f32[2,128]{1,0:T(2,128)S(1)}, f32[2,128]{1,0:T(2,128)}, u32[]{:S(2)}) copy-start(f32[2,128]{1,0:T(2,128)} %get-tuple-element.5) | copy-start | bytes 3076

commit v2 on v1

--- a/solution.py
+++ b/solution.py
@@ -12,9 +12,9 @@
 DIRS = tuple((dx, dy) for dx in (-1, 0, 1) for dy in (-1, 0, 1) if dx != 0 or dy != 0)
 
 
-def kernel(nb, ngx, ngy, disp, force, kappa, sigma, gap0, press, mortar, partner, active,
-           inc_out, np_out, f0, f1, f2, v2, diag, force_v, sigma_v, mort, surf, usend, urecv,
-           gsend, grecv, cols, load_sem, hs, hr, ss, sr, us, ur, gs, gr):
+def kernel(nb, ngx, ngy, disp, force, kappa, sigma, gap0_in, press_in, mortar, partner_in, active_in,
+           inc_out, np_out, gap0, press, partner, active, f0, f1, f2, v2, diag, force_v, sigma_v, mort, surf, usend, urecv,
+           grecv, final, cols, load_sem, hs, hr, ss, sr, us, ur, gs, gr, fs, fr):
     comp, cx, cy, nz = force_v.shape
     bpd, sblk = gap0.shape
     per = sblk // cy
@@ -28,6 +28,10 @@
         pltpu.make_async_copy(mortar, mort, load_sem.at[2]),
         pltpu.make_async_copy(sigma.at[0], sigma_v, load_sem.at[3]),
         pltpu.make_async_copy(force.at[0], force_v, load_sem.at[4]),
+        pltpu.make_async_copy(gap0_in, gap0, load_sem.at[5]),
+        pltpu.make_async_copy(press_in, press, load_sem.at[6]),
+        pltpu.make_async_copy(partner_in, partner, load_sem.at[7]),
+        pltpu.make_async_copy(active_in, active, load_sem.at[8]),
     ]
     for load in loads:
         load.start()
@@ -43,14 +47,6 @@
         if dy > 0:
             good = good & (gy < ngy - 1)
         return good
-
-    for f in (f0, f1, f2):
-        for c in range(f.shape[0]):
-            for x in (0, cx + 1):
-                f[c, x] = jnp.zeros(f.shape[2:], f.dtype)
-            for x in range(1, cx + 1):
-                f[c, x, YB - 1 : YB] = jnp.zeros((1, nz), f.dtype)
-                f[c, x, YB + cy : YB + cy + 1] = jnp.zeros((1, nz), f.dtype)
 
     row_peers = [(db, k) for db in range(nb) for k in range(ngx) if db or k]
     barrier = pltpu.get_barrier_semaphore()
@@ -68,6 +64,22 @@
             @pl.when(here)
             def _():
                 pl.semaphore_signal(barrier, inc=1, device_id={"gx": gx + dx, "gy": gy + dy}, device_id_type=MESH)
+
+    for side, x in ((-1, 0), (1, cx + 1)):
+        @pl.when(jnp.logical_not(exists(side, 0)))
+        def _():
+            for f in (f0, f1, f2):
+                for c in range(f.shape[0]):
+                    f[c, x, YB - 1 : YB] = jnp.zeros((1, nz), f.dtype)
+                    f[c, x, YB : YB + cy] = jnp.zeros((cy, nz), f.dtype)
+                    f[c, x, YB + cy : YB + cy + 1] = jnp.zeros((1, nz), f.dtype)
+    for side, y in ((-1, YB - 1), (1, YB + cy)):
+        @pl.when(jnp.logical_not(exists(0, side)))
+        def _():
+            for f in (f0, f1, f2):
+                for c in range(f.shape[0]):
+                    for x in range(cx + 2):
+                        f[c, x, y : y + 1] = jnp.zeros((1, nz), f.dtype)
 
     lane = lax.broadcasted_iota(jnp.int32, (sblk, nz), 1)
     eye = lax.broadcasted_iota(jnp.int32, (sblk, nz), 0) == lane
@@ -131,13 +143,21 @@
             src_ref=surf.at[r, wb, wg], dst_ref=surf.at[r, wb, wg], send_sem=ss.at[r, i],
             recv_sem=sr.at[r, wb * ngx + wg], device_id={"body": ob, "gx": og}, device_id_type=MESH)
 
+    def surf_each(r, incoming, act):
+        for i, (db, k) in enumerate(row_peers):
+            def go():
+                act(surf_copy(r, i, db, k, incoming))
+            if r >= 2 or (db == 1 and k == 0):
+                go()
+            else:
+                origin = lax.rem(b + db, nb) if incoming else b
+                pl.when(origin == 1)(go)
+
     def surf_send(r):
-        for i, (db, k) in enumerate(row_peers):
-            surf_copy(r, i, db, k, False).start()
+        surf_each(r, False, lambda copy: copy.start())
 
     def surf_wait(r):
-        for i, (db, k) in enumerate(row_peers):
-            surf_copy(r, i, db, k, True).wait_recv()
+        surf_each(r, True, lambda copy: copy.wait_recv())
 
     def u_copy(r, k, incoming):
         og = lax.rem(gx + k, ngx)
@@ -152,23 +172,42 @@
             src_ref=grecv.at[s, w], dst_ref=grecv.at[s, w], send_sem=gs.at[s, k], recv_sem=gr.at[s, w],
             device_id={"gy": og}, device_id_type=MESH)
 
-    def g_send(s, r):
-        total = surf[r, 0, 0]
+    def scalars(total):
+        return (jnp.sum(total[0:1, :], axis=1, keepdims=True), jnp.sum(total[1:2, :], axis=1, keepdims=True))
+
+    def g_send():
+        total = surf[2, 0, 0, bpd : bpd + 2, :]
         for w in range(1, nb * ngx):
-            total = total + surf[r, w // ngx, w % ngx]
-        grecv[s, gy] = total
+            total = total + surf[2, w // ngx, w % ngx, bpd : bpd + 2, :]
+        grecv[0, gy] = total
         for k in range(1, ngy):
-            g_copy(s, k, False).start()
-
-    def g_take(s):
+            g_copy(0, k, False).start()
+
+    def g_take():
         for k in range(1, ngy):
-            g_copy(s, k, True).wait_recv()
-        total = grecv[s, 0]
+            g_copy(0, k, True).wait_recv()
+        total = grecv[0, 0]
         for w in range(1, ngy):
-            total = total + grecv[s, w]
-        norm = jnp.sum(total[bpd : bpd + 1, :], axis=1, keepdims=True)
-        product = jnp.sum(total[bpd + 1 : bpd + 2, :], axis=1, keepdims=True)
-        return norm, product
+            total = total + grecv[0, w]
+        return scalars(total)
+
+    count = nb * ngx * ngy
+    me = (b * ngx + gx) * ngy + gy
+
+    def each_peer(act):
+        if count <= 64:
+            for k in range(1, count):
+                act(k)
+        else:
+            pl.loop(1, count)(act)
+
+    def final_copy(k, incoming):
+        other = lax.rem(me + k, count)
+        w = other if incoming else me
+        return pltpu.make_async_remote_copy(
+            src_ref=final.at[w], dst_ref=final.at[w], send_sem=fs.at[k], recv_sem=fr.at[w],
+            device_id={"body": other // (ngx * ngy), "gx": lax.rem(other // ngy, ngx), "gy": lax.rem(other, ngy)},
+            device_id_type=MESH)
 
     def b_of(r, l):
         picked = jnp.zeros((1, sblk), jnp.float32)
@@ -194,6 +233,8 @@
 
     def u_finish(r, f, x0, y0):
         def add(l, col):
+            if f is None:
+                return
             xs = slice(x0 + l * per, x0 + (l + 1) * per)
             block = f[comp - 1, xs, y0 : y0 + cy, :].reshape(sblk, nz)
             f[comp - 1, xs, y0 : y0 + cy, :] = (block - jnp.where(first_lane, col, 0.0)).reshape(per, cy, nz)
@@ -201,6 +242,7 @@
         @pl.when(b == 0)
         def _():
             for l in range(bpd):
+                cols[6, l] = cols[5, l]
                 add(l, cols[5, l])
 
         @pl.when(b == 1)
@@ -212,7 +254,9 @@
                 row = urecv[r, 0, l : l + 1, :]
                 for g in range(1, ngx):
                     row = row + urecv[r, g, l : l + 1, :]
-                add(l, to_col(row))
+                col = to_col(row)
+                cols[6, l] = col
+                add(l, col)
 
     def apply(f, emit):
         @pl.loop(0, comp)
@@ -234,7 +278,6 @@
     loads[1].wait()
     surf[0, b, gx] = jnp.zeros(surf.shape[3:], jnp.float32)
     surface_rows(f0, 0)
-    usend[...] = jnp.zeros(usend.shape, jnp.float32)
     pl.semaphore_wait(barrier, expect)
 
     surf_send(0)
@@ -286,17 +329,23 @@
         f2[c, 1 + x, YB : YB + cy, :] = val
 
     apply(f1, emit_v1)
-    u_finish(1, f2, 1, YB)
-
-    def sums(left, right):
-        norm = jnp.zeros((cy, nz), jnp.float32)
-        product = jnp.zeros((cy, nz), jnp.float32)
+
+    def sum_of(left, right):
+        total = jnp.zeros((cy, nz), jnp.float32)
         for c in range(comp):
             for x in range(cx):
-                a, m = left(c, x), right(c, x)
-                norm = norm + a * a
-                product = product + a * m
-        return jnp.sum(norm, axis=0, keepdims=True), jnp.sum(product, axis=0, keepdims=True)
+                total = total + left(c, x) * right(c, x)
+        return jnp.sum(total, axis=0, keepdims=True)
+
+    def surface_col(value, l):
+        return jnp.concatenate([value(comp - 1, l * per + i) for i in range(per)], axis=0)
+
+    def surface_sum(left, right_cols):
+        total = jnp.zeros((1, nz), jnp.float32)
+        for l in range(bpd):
+            term = jnp.where(first_lane, surface_col(left, l) * right_cols[l], 0.0)
+            total = total + jnp.sum(term, axis=0, keepdims=True)
+        return total
 
     def r0_of(c, x):
         return f1[c, 1 + x, YB : YB + cy, :]
@@ -304,15 +353,19 @@
     def v1_of(c, x):
         return f2[c, 1 + x, YB : YB + cy, :]
 
+    norm = sum_of(r0_of, r0_of)
+    product = sum_of(r0_of, v1_of)
+    u_finish(1, f2, 1, YB)
+    product = product - surface_sum(r0_of, [cols[6, l] for l in range(bpd)])
+
     surf[2, b, gx] = jnp.zeros(surf.shape[3:], jnp.float32)
-    norm, product = sums(r0_of, v1_of)
     surf[2, b, gx, bpd : bpd + 1, :] = norm
     surf[2, b, gx, bpd + 1 : bpd + 2, :] = product
     surface_rows(f2, 2)
     surf_send(2)
     halo_send(f2, 2)
     surf_wait(2)
-    g_send(0, 2)
+    g_send()
     for l in range(bpd):
         gap = b_of(2, l)
         cols[4, l] = gap
@@ -324,19 +377,21 @@
         v2[c, x] = val
 
     apply(f2, emit_v2)
-    u_finish(2, v2, 0, 0)
-    norm0, product0 = g_take(0)
+    norm0, product0 = g_take()
     alpha0 = norm0 / product0
 
-    norm, product = sums(lambda c, x: r0_of(c, x) - alpha0 * v1_of(c, x),
-                         lambda c, x: v1_of(c, x) - alpha0 * v2[c, x])
-    surf[3, b, gx] = jnp.zeros(surf.shape[3:], jnp.float32)
-    surf[3, b, gx, bpd : bpd + 1, :] = norm
-    surf[3, b, gx, bpd + 1 : bpd + 2, :] = product
-    surf_send(3)
-    surf_wait(3)
-    g_send(1, 3)
-    norm1, product1 = g_take(1)
+    def r1_of(c, x):
+        return r0_of(c, x) - alpha0 * v1_of(c, x)
+
+    norm = sum_of(r1_of, r1_of)
+    product = sum_of(r1_of, lambda c, x: v1_of(c, x) - alpha0 * v2[c, x])
+    u_finish(2, None, 0, 0)
+    product = product + alpha0 * surface_sum(r1_of, [cols[6, l] for l in range(bpd)])
+    final[me, 0:1, :] = norm
+    final[me, 1:2, :] = product
+    each_peer(lambda k: final_copy(k, False).start())
+    each_peer(lambda k: final_copy(k, True).wait_recv())
+    norm1, product1 = scalars(lax.fori_loop(1, count, lambda w, t: t + final[w], final[0], unroll=count <= 64))
     ratio = norm1 / norm0
     alpha1 = norm1 / (product1 - ratio * norm1 / alpha0)
     coef_r = alpha0 + alpha1 * (1.0 + ratio)
@@ -352,12 +407,11 @@
 
     for r, f in enumerate((f0, f1, f2)):
         halo_done(f, r)
-    for r in range(4):
-        for i, (db, k) in enumerate(row_peers):
-            surf_copy(r, i, db, k, False).wait_send()
-    for s in range(2):
-        for k in range(1, ngy):
-            g_copy(s, k, False).wait_send()
+    for r in range(3):
+        surf_each(r, False, lambda copy: copy.wait_send())
+    for k in range(1, ngy):
+        g_copy(0, k, False).wait_send()
+    each_peer(lambda k: final_copy(k, False).wait_send())
 
     @pl.when(b == 1)
     def _():
@@ -373,15 +427,18 @@
     f32 = jnp.float32
     any_spec = pl.BlockSpec(memory_space=pl.ANY)
     vmem = pl.BlockSpec(memory_space=pltpu.VMEM)
-    smem = pl.BlockSpec(memory_space=pltpu.SMEM)
     rows = cy + 2 * YB
     dma = pltpu.SemaphoreType.DMA
     return pl.pallas_call(
         functools.partial(kernel, nb, ngx, ngy),
         out_shape=(jax.ShapeDtypeStruct(disp.shape, f32), jax.ShapeDtypeStruct(gap0.shape, f32)),
-        in_specs=[any_spec, any_spec, any_spec, any_spec, vmem, vmem, any_spec, smem, smem],
+        in_specs=[any_spec] * 9,
         out_specs=(vmem, vmem),
         scratch_shapes=[
+            pltpu.VMEM((bpd, sblk), f32),
+            pltpu.VMEM((bpd, sblk), f32),
+            pltpu.SMEM((bpd,), jnp.int32),
+            pltpu.SMEM((bpd,), jnp.int32),
             pltpu.VMEM((comp + 1, cx + 2, rows, nz), f32),
             pltpu.VMEM((comp, cx + 2, rows, nz), f32),
             pltpu.VMEM((comp, cx + 2, rows, nz), f32),
@@ -390,17 +447,18 @@
             pltpu.VMEM((comp, cx, cy, nz), f32),
             pltpu.VMEM((cx, cy, nz), f32),
             pltpu.VMEM((bpd, sblk, sblk), f32),
-            pltpu.VMEM((4, nb, ngx, 8, sblk), f32),
-            pltpu.VMEM((3, ngx, 8, sblk), f32),
-            pltpu.VMEM((3, ngx, 8, sblk), f32),
-            pltpu.VMEM((8, sblk), f32),
-            pltpu.VMEM((2, ngy, 8, sblk), f32),
-            pltpu.VMEM((6, bpd, sblk, 1), f32),
-            dma((5,)),
+            pltpu.VMEM((3, nb, ngx, bpd + 2, sblk), f32),
+            pltpu.VMEM((3, ngx, bpd, sblk), f32),
+            pltpu.VMEM((3, ngx, bpd, sblk), f32),
+            pltpu.VMEM((1, ngy, 2, sblk), f32),
+            pltpu.VMEM((nb * ngx * ngy, 2, sblk), f32),
+            pltpu.VMEM((7, bpd, sblk, 1), f32),
+            dma((9,)),
             dma((3, len(DIRS))), dma((3, len(DIRS))),
-            dma((4, nb * ngx)), dma((4, nb * ngx)),
+            dma((3, nb * ngx)), dma((3, nb * ngx)),
             dma((3, ngx)), dma((3, ngx)),
-            dma((2, ngy)), dma((2, ngy)),
+            dma((1, ngy)), dma((1, ngy)),
+            dma((nb * ngx * ngy,)), dma((nb * ngx * ngy,)),
         ],
         compiler_params=pltpu.CompilerParams(collective_id=0, has_side_effects=True,
                                              vmem_limit_bytes=60 * 1024 * 1024),

time: 37.6 us -> 34.2 us (0.910)
  Pallas kernels: 34.5 us -> 31.1 us
    pallas_call x1, Pallas kernels: 34.5 us -> 31.1 us  [on_device(): pl.pallas_call(functools.partial(kernel, nb, ngx, ngy), out_shape=(jax.Sh...]
where the time goes in v2:
time: 34.2 us; the launch traced here: 34.1 us
  Pallas kernels  31.1 us (91%)
  local copies, waits for them, and re-layouts  2.33 us (7%)
  between operations  0.65 us (2%)
    pallas_call x1, Pallas kernels, on_device(): pl.pallas_call(functools.partial(kernel, nb, ngx, ngy), out_shape=(jax.Sh...  31.1 us
    unnamed x4, local copies, waits for them, and re-layouts  2.33 us

profile of v2, /device:TPU:0, one launch (start us, length us, event | category | flops | bytes accessed | tf_op | source)
XLA Modules:
  0.0 34.1 jit_solution(13288724791712880106)
XLA Ops:
  0.6 31.1 %newton_step.1 = (f32[1,3,8,32,128]{4,3,2,1,0:T(8,128)}, f32[2,128]{1,0:T(2,128)}) custom-call(f32[1,3,8,32,128]{4,3,2,1,0:T(8,128)} %disp.1, f32[1,3,8,32,128]{4,3,2,1,0:T(8,128)} %force.1, f32[1,8,32,128]{3,2,1,0:T(8,128)} %kappa.1, f32[1,8,32,128]{3,2,1,0:T(8,128)} %sigma.1, f32[2,128]{1,0:T(2,128)} %gap0_in.1, f32[2,128]{1,0:T(2,128)} %press_in.1, ...), custom_call_target="tpu_custom_call" | custom-call | tf_op jit(solution)/shard_map/newton_step/pallas_call | solution.py:432
  31.7 0.0 copy-start
  31.7 1.8 %copy.13 = f32[1,3,8,32,128]{4,3,2,1,0:T(8,128)} copy(f32[1,3,8,32,128]{4,3,2,1,0:T(8,128)} %get-tuple-element.4) | data formatting | bytes 786432
  33.5 0.0 copy-done
  33.5 0.6 %copy.14 = f32[2,128]{1,0:T(2,128)} copy(f32[2,128]{1,0:T(2,128)S(1)} %copy-done) | data formatting | bytes 2048
Async XLA Ops:
  31.7 1.8 %copy-start = (f32[2,128]{1,0:T(2,128)S(1)}, f32[2,128]{1,0:T(2,128)}, u32[]{:S(2)}) copy-start(f32[2,128]{1,0:T(2,128)} %get-tuple-element.5) | copy-start | bytes 3076

commit v3 on v2

--- a/solution.py
+++ b/solution.py
@@ -14,7 +14,7 @@
 
 def kernel(nb, ngx, ngy, disp, force, kappa, sigma, gap0_in, press_in, mortar, partner_in, active_in,
            inc_out, np_out, gap0, press, partner, active, f0, f1, f2, v2, diag, force_v, sigma_v, mort, surf, usend, urecv,
-           grecv, final, cols, load_sem, hs, hr, ss, sr, us, ur, gs, gr, fs, fr):
+           dots, grecv, final, cols, load_sem, hs, hr, ss, sr, us, ur, ds, dr, gs, gr, fs, fr):
     comp, cx, cy, nz = force_v.shape
     bpd, sblk = gap0.shape
     per = sblk // cy
@@ -147,7 +147,7 @@
         for i, (db, k) in enumerate(row_peers):
             def go():
                 act(surf_copy(r, i, db, k, incoming))
-            if r >= 2 or (db == 1 and k == 0):
+            if db == 1 and k == 0:
                 go()
             else:
                 origin = lax.rem(b + db, nb) if incoming else b
@@ -175,10 +175,19 @@
     def scalars(total):
         return (jnp.sum(total[0:1, :], axis=1, keepdims=True), jnp.sum(total[1:2, :], axis=1, keepdims=True))
 
+    def dot_copy(i, db, k, incoming):
+        ob, og = lax.rem(b + db, nb), lax.rem(gx + k, ngx)
+        wb, wg = (ob, og) if incoming else (b, gx)
+        return pltpu.make_async_remote_copy(
+            src_ref=dots.at[wb, wg], dst_ref=dots.at[wb, wg], send_sem=ds.at[i],
+            recv_sem=dr.at[wb * ngx + wg], device_id={"body": ob, "gx": og}, device_id_type=MESH)
+
     def g_send():
-        total = surf[2, 0, 0, bpd : bpd + 2, :]
+        for i, (db, k) in enumerate(row_peers):
+            dot_copy(i, db, k, True).wait_recv()
+        total = dots[0, 0]
         for w in range(1, nb * ngx):
-            total = total + surf[2, w // ngx, w % ngx, bpd : bpd + 2, :]
+            total = total + dots[w // ngx, w % ngx]
         grecv[0, gy] = total
         for k in range(1, ngy):
             g_copy(0, k, False).start()
@@ -231,18 +240,15 @@
             for k in range(1, ngx):
                 u_copy(r, k, False).start()
 
-    def u_finish(r, f, x0, y0):
+    def u_finish(r, f):
         def add(l, col):
-            if f is None:
-                return
-            xs = slice(x0 + l * per, x0 + (l + 1) * per)
-            block = f[comp - 1, xs, y0 : y0 + cy, :].reshape(sblk, nz)
-            f[comp - 1, xs, y0 : y0 + cy, :] = (block - jnp.where(first_lane, col, 0.0)).reshape(per, cy, nz)
+            xs = slice(1 + l * per, 1 + (l + 1) * per)
+            block = f[comp - 1, xs, YB : YB + cy, :].reshape(sblk, nz)
+            f[comp - 1, xs, YB : YB + cy, :] = (block - jnp.where(first_lane, col, 0.0)).reshape(per, cy, nz)
 
         @pl.when(b == 0)
         def _():
             for l in range(bpd):
-                cols[6, l] = cols[5, l]
                 add(l, cols[5, l])
 
         @pl.when(b == 1)
@@ -254,9 +260,7 @@
                 row = urecv[r, 0, l : l + 1, :]
                 for g in range(1, ngx):
                     row = row + urecv[r, g, l : l + 1, :]
-                col = to_col(row)
-                cols[6, l] = col
-                add(l, col)
+                add(l, to_col(row))
 
     def apply(f, emit):
         @pl.loop(0, comp)
@@ -276,7 +280,6 @@
 
     loads[0].wait()
     loads[1].wait()
-    surf[0, b, gx] = jnp.zeros(surf.shape[3:], jnp.float32)
     surface_rows(f0, 0)
     pl.semaphore_wait(barrier, expect)
 
@@ -311,9 +314,8 @@
         f1[c, 1 + x, YB : YB + cy, :] = force_v[c, x] - val
 
     apply(f0, emit_rhs)
-    u_finish(0, f1, 1, YB)
-
-    surf[1, b, gx] = jnp.zeros(surf.shape[3:], jnp.float32)
+    u_finish(0, f1)
+
     surface_rows(f1, 1)
     surf_send(1)
     halo_send(f1, 1)
@@ -337,15 +339,14 @@
                 total = total + left(c, x) * right(c, x)
         return jnp.sum(total, axis=0, keepdims=True)
 
-    def surface_col(value, l):
-        return jnp.concatenate([value(comp - 1, l * per + i) for i in range(per)], axis=0)
-
-    def surface_sum(left, right_cols):
-        total = jnp.zeros((1, nz), jnp.float32)
+    first_row = lax.broadcasted_iota(jnp.int32, (1, nz), 1) == 0
+    slave_side = (b == 0).astype(jnp.float32)
+
+    def contact_sum(left, right):
+        total = jnp.zeros((1, 1), jnp.float32)
         for l in range(bpd):
-            term = jnp.where(first_lane, surface_col(left, l) * right_cols[l], 0.0)
-            total = total + jnp.sum(term, axis=0, keepdims=True)
-        return total
+            total = total + jnp.sum(cols[0, l] * left(l) * right(l), axis=0, keepdims=True)
+        return jnp.where(first_row, slave_side * total, 0.0)
 
     def r0_of(c, x):
         return f1[c, 1 + x, YB : YB + cy, :]
@@ -353,24 +354,19 @@
     def v1_of(c, x):
         return f2[c, 1 + x, YB : YB + cy, :]
 
-    norm = sum_of(r0_of, r0_of)
-    product = sum_of(r0_of, v1_of)
-    u_finish(1, f2, 1, YB)
-    product = product - surface_sum(r0_of, [cols[6, l] for l in range(bpd)])
-
-    surf[2, b, gx] = jnp.zeros(surf.shape[3:], jnp.float32)
-    surf[2, b, gx, bpd : bpd + 1, :] = norm
-    surf[2, b, gx, bpd + 1 : bpd + 2, :] = product
+    dots[b, gx, 0:1, :] = sum_of(r0_of, r0_of)
+    dots[b, gx, 1:2, :] = sum_of(r0_of, v1_of) + contact_sum(lambda l: cols[3, l], lambda l: cols[3, l])
+    for i, (db, k) in enumerate(row_peers):
+        dot_copy(i, db, k, False).start()
+    u_finish(1, f2)
+
     surface_rows(f2, 2)
     surf_send(2)
     halo_send(f2, 2)
+    g_send()
     surf_wait(2)
-    g_send()
     for l in range(bpd):
-        gap = b_of(2, l)
-        cols[4, l] = gap
-        cols[5, l] = cols[0, l] * gap
-    u_start(2)
+        cols[4, l] = b_of(2, l)
     halo_wait(f2, 2)
 
     def emit_v2(c, x, val):
@@ -385,8 +381,7 @@
 
     norm = sum_of(r1_of, r1_of)
     product = sum_of(r1_of, lambda c, x: v1_of(c, x) - alpha0 * v2[c, x])
-    u_finish(2, None, 0, 0)
-    product = product + alpha0 * surface_sum(r1_of, [cols[6, l] for l in range(bpd)])
+    product = product - alpha0 * contact_sum(lambda l: cols[3, l] - alpha0 * cols[4, l], lambda l: cols[4, l])
     final[me, 0:1, :] = norm
     final[me, 1:2, :] = product
     each_peer(lambda k: final_copy(k, False).start())
@@ -409,13 +404,15 @@
         halo_done(f, r)
     for r in range(3):
         surf_each(r, False, lambda copy: copy.wait_send())
+    for i, (db, k) in enumerate(row_peers):
+        dot_copy(i, db, k, False).wait_send()
     for k in range(1, ngy):
         g_copy(0, k, False).wait_send()
     each_peer(lambda k: final_copy(k, False).wait_send())
 
     @pl.when(b == 1)
     def _():
-        for r in range(3):
+        for r in range(2):
             for k in range(1, ngx):
                 u_copy(r, k, False).wait_send()
 
@@ -431,7 +428,7 @@
     dma = pltpu.SemaphoreType.DMA
     return pl.pallas_call(
         functools.partial(kernel, nb, ngx, ngy),
-        out_shape=(jax.ShapeDtypeStruct(disp.shape, f32), jax.ShapeDtypeStruct(gap0.shape, f32)),
+        out_shape=(pltpu.VMEM(disp.shape, f32), pltpu.VMEM(gap0.shape, f32)),
         in_specs=[any_spec] * 9,
         out_specs=(vmem, vmem),
         scratch_shapes=[
@@ -447,16 +444,18 @@
             pltpu.VMEM((comp, cx, cy, nz), f32),
             pltpu.VMEM((cx, cy, nz), f32),
             pltpu.VMEM((bpd, sblk, sblk), f32),
-            pltpu.VMEM((3, nb, ngx, bpd + 2, sblk), f32),
-            pltpu.VMEM((3, ngx, bpd, sblk), f32),
-            pltpu.VMEM((3, ngx, bpd, sblk), f32),
+            pltpu.VMEM((3, nb, ngx, bpd, sblk), f32),
+            pltpu.VMEM((2, ngx, bpd, sblk), f32),
+            pltpu.VMEM((2, ngx, bpd, sblk), f32),
+            pltpu.VMEM((nb, ngx, 2, sblk), f32),
             pltpu.VMEM((1, ngy, 2, sblk), f32),
             pltpu.VMEM((nb * ngx * ngy, 2, sblk), f32),
-            pltpu.VMEM((7, bpd, sblk, 1), f32),
+            pltpu.VMEM((6, bpd, sblk, 1), f32),
             dma((9,)),
             dma((3, len(DIRS))), dma((3, len(DIRS))),
             dma((3, nb * ngx)), dma((3, nb * ngx)),
-            dma((3, ngx)), dma((3, ngx)),
+            dma((2, ngx)), dma((2, ngx)),
+            dma((nb * ngx,)), dma((nb * ngx,)),
             dma((1, ngy)), dma((1, ngy)),
             dma((nb * ngx * ngy,)), dma((nb * ngx * ngy,)),
         ],

time: 34.2 us -> 30.8 us (0.901)
  Pallas kernels: 31.1 us -> 28.7 us
  local copies, waits for them, and re-layouts: 2.33 us -> 1.31 us
    pallas_call x1, Pallas kernels: 31.1 us -> 28.7 us  [on_device(): pl.pallas_call(functools.partial(kernel, nb, ngx, ngy), out_shape=(pltpu....]
    unnamed x4 -> x2, local copies, waits for them, and re-layouts: 2.33 us -> 1.31 us
where the time goes in v3:
time: 30.8 us; the launch traced here: 30.7 us
  Pallas kernels  28.7 us (93%)
  local copies, waits for them, and re-layouts  1.31 us (4%)
  between operations  0.64 us (2%)
    pallas_call x1, Pallas kernels, on_device(): pl.pallas_call(functools.partial(kernel, nb, ngx, ngy), out_shape=(pltpu....  28.7 us
    unnamed x2, local copies, waits for them, and re-layouts  1.31 us

profile of v3, /device:TPU:0, one launch (start us, length us, event | category | flops | bytes accessed | tf_op | source)
XLA Modules:
  0.0 30.7 jit_solution(7587292196173352966)
XLA Ops:
  0.6 28.7 %newton_step.1 = (f32[1,3,8,32,128]{4,3,2,1,0:T(8,128)S(1)}, f32[2,128]{1,0:T(2,128)S(1)}) custom-call(f32[1,3,8,32,128]{4,3,2,1,0:T(8,128)} %disp.1, f32[1,3,8,32,128]{4,3,2,1,0:T(8,128)} %force.1, f32[1,8,32,128]{3,2,1,0:T(8,128)} %kappa.1, f32[1,8,32,128]{3,2,1,0:T(8,128)} %sigma.1, f32[2,128]{1,0:T(2,128)} %gap0_in.1, f32[2,128]{1,0:T(2,128)} %press_in.1, ...), custom_call_target="tpu_custom_call" | custom-call | tf_op jit(solution)/shard_map/newton_step/pallas_call | solution.py:429
  29.4 0.7 %copy.13 = f32[1,3,8,32,128]{4,3,2,1,0:T(8,128)} copy(f32[1,3,8,32,128]{4,3,2,1,0:T(8,128)S(1)} %get-tuple-element.2) | data formatting | bytes 786432
  30.1 0.6 %copy.14 = f32[2,128]{1,0:T(2,128)} copy(f32[2,128]{1,0:T(2,128)S(1)} %get-tuple-element.3) | data formatting | bytes 2048

commit v4 on v3

--- a/solution.py
+++ b/solution.py
@@ -14,7 +14,7 @@
 
 def kernel(nb, ngx, ngy, disp, force, kappa, sigma, gap0_in, press_in, mortar, partner_in, active_in,
            inc_out, np_out, gap0, press, partner, active, f0, f1, f2, v2, diag, force_v, sigma_v, mort, surf, usend, urecv,
-           dots, grecv, final, cols, load_sem, hs, hr, ss, sr, us, ur, ds, dr, gs, gr, fs, fr):
+           final, cols, load_sem, hs, hr, ss, sr, us, ur, fs, fr):
     comp, cx, cy, nz = force_v.shape
     bpd, sblk = gap0.shape
     per = sblk // cy
@@ -49,21 +49,37 @@
         return good
 
     row_peers = [(db, k) for db in range(nb) for k in range(ngx) if db or k]
+    count = nb * ngx * ngy
+    me = (b * ngx + gx) * ngy + gy
+
+    def place_of(other):
+        return {"body": other // (ngx * ngy), "gx": lax.rem(other // ngy, ngx), "gy": lax.rem(other, ngy)}
+
+    def each_peer(act):
+        if count <= 64:
+            for k in range(1, count):
+                act(k)
+        else:
+            pl.loop(1, count)(act)
+
     barrier = pltpu.get_barrier_semaphore()
-    for db, k in row_peers:
-        pl.semaphore_signal(barrier, inc=1, device_id={"body": lax.rem(b + db, nb), "gx": lax.rem(gx + k, ngx)},
-                            device_id_type=MESH)
-    for k in range(1, ngy):
-        pl.semaphore_signal(barrier, inc=1, device_id={"gy": lax.rem(gy + k, ngy)}, device_id_type=MESH)
-    expect = len(row_peers) + ngy - 1
-    for dx, dy in DIRS:
-        if dx and dy:
-            here = exists(dx, dy)
-            expect = expect + here.astype(jnp.int32)
-
-            @pl.when(here)
-            def _():
-                pl.semaphore_signal(barrier, inc=1, device_id={"gx": gx + dx, "gy": gy + dy}, device_id_type=MESH)
+    if ngy <= 4:
+        for db, k in row_peers:
+            pl.semaphore_signal(barrier, inc=1, device_id={"body": lax.rem(b + db, nb), "gx": lax.rem(gx + k, ngx)},
+                                device_id_type=MESH)
+        expect = len(row_peers)
+        for dx, dy in DIRS:
+            if dy:
+                here = exists(dx, dy)
+                expect = expect + here.astype(jnp.int32)
+
+                @pl.when(here)
+                def _():
+                    pl.semaphore_signal(barrier, inc=1, device_id={"gx": gx + dx, "gy": gy + dy}, device_id_type=MESH)
+    else:
+        each_peer(lambda k: pl.semaphore_signal(barrier, inc=1, device_id=place_of(lax.rem(me + k, count)),
+                                                device_id_type=MESH))
+        expect = count - 1
 
     for side, x in ((-1, 0), (1, cx + 1)):
         @pl.when(jnp.logical_not(exists(side, 0)))
@@ -165,57 +181,12 @@
             src_ref=usend.at[r, og], dst_ref=urecv.at[r, og if incoming else gx], send_sem=us.at[r, k],
             recv_sem=ur.at[r, og if incoming else gx], device_id={"gx": og}, device_id_type=MESH)
 
-    def g_copy(s, k, incoming):
-        og = lax.rem(gy + k, ngy)
-        w = og if incoming else gy
-        return pltpu.make_async_remote_copy(
-            src_ref=grecv.at[s, w], dst_ref=grecv.at[s, w], send_sem=gs.at[s, k], recv_sem=gr.at[s, w],
-            device_id={"gy": og}, device_id_type=MESH)
-
-    def scalars(total):
-        return (jnp.sum(total[0:1, :], axis=1, keepdims=True), jnp.sum(total[1:2, :], axis=1, keepdims=True))
-
-    def dot_copy(i, db, k, incoming):
-        ob, og = lax.rem(b + db, nb), lax.rem(gx + k, ngx)
-        wb, wg = (ob, og) if incoming else (b, gx)
-        return pltpu.make_async_remote_copy(
-            src_ref=dots.at[wb, wg], dst_ref=dots.at[wb, wg], send_sem=ds.at[i],
-            recv_sem=dr.at[wb * ngx + wg], device_id={"body": ob, "gx": og}, device_id_type=MESH)
-
-    def g_send():
-        for i, (db, k) in enumerate(row_peers):
-            dot_copy(i, db, k, True).wait_recv()
-        total = dots[0, 0]
-        for w in range(1, nb * ngx):
-            total = total + dots[w // ngx, w % ngx]
-        grecv[0, gy] = total
-        for k in range(1, ngy):
-            g_copy(0, k, False).start()
-
-    def g_take():
-        for k in range(1, ngy):
-            g_copy(0, k, True).wait_recv()
-        total = grecv[0, 0]
-        for w in range(1, ngy):
-            total = total + grecv[0, w]
-        return scalars(total)
-
-    count = nb * ngx * ngy
-    me = (b * ngx + gx) * ngy + gy
-
-    def each_peer(act):
-        if count <= 64:
-            for k in range(1, count):
-                act(k)
-        else:
-            pl.loop(1, count)(act)
-
     def final_copy(k, incoming):
         other = lax.rem(me + k, count)
         w = other if incoming else me
         return pltpu.make_async_remote_copy(
             src_ref=final.at[w], dst_ref=final.at[w], send_sem=fs.at[k], recv_sem=fr.at[w],
-            device_id={"body": other // (ngx * ngy), "gx": lax.rem(other // ngy, ngx), "gy": lax.rem(other, ngy)},
+            device_id=place_of(other),
             device_id_type=MESH)
 
     def b_of(r, l):
@@ -292,15 +263,16 @@
         gap = to_col(gap0[l : l + 1, :]) + b_of(0, l)
         prs = to_col(press[l : l + 1, :])
         radius = jnp.sqrt(gap * gap + prs * prs + 0.01)
+        per_radius = 1.0 / radius
         complement = gap + prs - radius
-        slope_gap = 1.0 - gap / radius
-        divisor = (1.0 - prs / radius) + 0.5
+        per_divisor = 1.0 / ((1.0 - prs * per_radius) + 0.5)
         flag = active[l].astype(jnp.float32)
-        cols[0, l] = flag * slope_gap / divisor
-        cols[1, l] = complement / divisor
-        cols[2, l] = slope_gap / divisor
-        cols[5, l] = flag * prs - flag * complement / divisor
+        cols[1, l] = complement * per_divisor
+        cols[2, l] = (1.0 - gap * per_radius) * per_divisor
+        cols[5, l] = flag * (prs - complement * per_divisor)
     u_start(0)
+    for l in range(bpd):
+        cols[0, l] = active[l].astype(jnp.float32) * cols[2, l]
     halo_wait(f0, 0)
     window = []
     for x in range(cx + 2):
@@ -337,16 +309,15 @@
         for c in range(comp):
             for x in range(cx):
                 total = total + left(c, x) * right(c, x)
-        return jnp.sum(total, axis=0, keepdims=True)
-
-    first_row = lax.broadcasted_iota(jnp.int32, (1, nz), 1) == 0
+        return jnp.sum(jnp.sum(total, axis=0, keepdims=True), axis=1, keepdims=True)
+
     slave_side = (b == 0).astype(jnp.float32)
 
     def contact_sum(left, right):
         total = jnp.zeros((1, 1), jnp.float32)
         for l in range(bpd):
             total = total + jnp.sum(cols[0, l] * left(l) * right(l), axis=0, keepdims=True)
-        return jnp.where(first_row, slave_side * total, 0.0)
+        return slave_side * total
 
     def r0_of(c, x):
         return f1[c, 1 + x, YB : YB + cy, :]
@@ -354,16 +325,21 @@
     def v1_of(c, x):
         return f2[c, 1 + x, YB : YB + cy, :]
 
-    dots[b, gx, 0:1, :] = sum_of(r0_of, r0_of)
-    dots[b, gx, 1:2, :] = sum_of(r0_of, v1_of) + contact_sum(lambda l: cols[3, l], lambda l: cols[3, l])
-    for i, (db, k) in enumerate(row_peers):
-        dot_copy(i, db, k, False).start()
     u_finish(1, f2)
 
     surface_rows(f2, 2)
     surf_send(2)
     halo_send(f2, 2)
-    g_send()
+    rr = sum_of(r0_of, r0_of)
+    rv = sum_of(r0_of, v1_of)
+    vv = sum_of(v1_of, v1_of)
+    own = jnp.where(vv > 0.0, rv / jnp.where(vv > 0.0, vv, 1.0), 0.0)
+
+    def near_of(c, x):
+        return r0_of(c, x) - own * v1_of(c, x)
+
+    nn = sum_of(near_of, near_of)
+    nv = sum_of(near_of, v1_of)
     surf_wait(2)
     for l in range(bpd):
         cols[4, l] = b_of(2, l)
@@ -373,20 +349,40 @@
         v2[c, x] = val
 
     apply(f2, emit_v2)
-    norm0, product0 = g_take()
-    alpha0 = norm0 / product0
-
-    def r1_of(c, x):
-        return r0_of(c, x) - alpha0 * v1_of(c, x)
-
-    norm = sum_of(r1_of, r1_of)
-    product = sum_of(r1_of, lambda c, x: v1_of(c, x) - alpha0 * v2[c, x])
-    product = product - alpha0 * contact_sum(lambda l: cols[3, l] - alpha0 * cols[4, l], lambda l: cols[4, l])
-    final[me, 0:1, :] = norm
-    final[me, 1:2, :] = product
+    nw = sum_of(near_of, lambda c, x: v2[c, x]) + contact_sum(lambda l: cols[3, l] - own * cols[4, l], lambda l: cols[4, l])
+    vw = sum_of(v1_of, lambda c, x: v2[c, x]) + contact_sum(lambda l: cols[4, l], lambda l: cols[4, l])
+
+    lane_of = lax.broadcasted_iota(jnp.int32, (1, sblk), 1)
+    for i, number in enumerate((rr, rv, vv, nn, nv, nw, vw, own)):
+        final[me, i : i + 1, :] = jnp.where(lane_of == lax.rem(me, sblk), number, 0.0)
     each_peer(lambda k: final_copy(k, False).start())
+    for r, f in enumerate((f0, f1, f2)):
+        halo_done(f, r)
+    for r in range(3):
+        surf_each(r, False, lambda copy: copy.wait_send())
+    @pl.when(b == 1)
+    def _():
+        for r in range(2):
+            for k in range(1, ngx):
+                u_copy(r, k, False).wait_send()
+
     each_peer(lambda k: final_copy(k, True).wait_recv())
-    norm1, product1 = scalars(lax.fori_loop(1, count, lambda w, t: t + final[w], final[0], unroll=count <= 64))
+    groups = []
+    for start in range(0, count, sblk):
+        stop = min(start + sblk, count)
+        groups.append(lax.fori_loop(start + 1, stop, lambda w, t: t + final[w], final[start], unroll=count <= 64))
+
+    def over(act):
+        total = act(*[groups[0][i : i + 1, :] for i in range(8)])
+        for group in groups[1:]:
+            total = total + act(*[group[i : i + 1, :] for i in range(8)])
+        return jnp.sum(total, axis=1, keepdims=True)
+
+    norm0 = over(lambda rr, rv, vv, nn, nv, nw, vw, own: rr)
+    alpha0 = norm0 / over(lambda rr, rv, vv, nn, nv, nw, vw, own: rv)
+    norm1 = over(lambda rr, rv, vv, nn, nv, nw, vw, own: nn - (alpha0 - own) * (2.0 * nv - (alpha0 - own) * vv))
+    product1 = over(lambda rr, rv, vv, nn, nv, nw, vw, own:
+                    nv - (alpha0 - own) * vv - alpha0 * (nw - (alpha0 - own) * vw))
     ratio = norm1 / norm0
     alpha1 = norm1 / (product1 - ratio * norm1 / alpha0)
     coef_r = alpha0 + alpha1 * (1.0 + ratio)
@@ -399,22 +395,7 @@
         flag = active[l].astype(jnp.float32)
         step = to_row(cols[1, l] + cols[2, l] * change)
         np_out[l : l + 1, :] = flag * (press[l : l + 1, :] - step)
-
-    for r, f in enumerate((f0, f1, f2)):
-        halo_done(f, r)
-    for r in range(3):
-        surf_each(r, False, lambda copy: copy.wait_send())
-    for i, (db, k) in enumerate(row_peers):
-        dot_copy(i, db, k, False).wait_send()
-    for k in range(1, ngy):
-        g_copy(0, k, False).wait_send()
     each_peer(lambda k: final_copy(k, False).wait_send())
-
-    @pl.when(b == 1)
-    def _():
-        for r in range(2):
-            for k in range(1, ngx):
-                u_copy(r, k, False).wait_send()
 
 
 def on_device(disp, force, kappa, sigma, gap0, pressure, mortar, partner, active):
@@ -447,16 +428,12 @@
             pltpu.VMEM((3, nb, ngx, bpd, sblk), f32),
             pltpu.VMEM((2, ngx, bpd, sblk), f32),
             pltpu.VMEM((2, ngx, bpd, sblk), f32),
-            pltpu.VMEM((nb, ngx, 2, sblk), f32),
-            pltpu.VMEM((1, ngy, 2, sblk), f32),
-            pltpu.VMEM((nb * ngx * ngy, 2, sblk), f32),
+            pltpu.VMEM((nb * ngx * ngy, 8, sblk), f32),
             pltpu.VMEM((6, bpd, sblk, 1), f32),
             dma((9,)),
             dma((3, len(DIRS))), dma((3, len(DIRS))),
             dma((3, nb * ngx)), dma((3, nb * ngx)),
             dma((2, ngx)), dma((2, ngx)),
-            dma((nb * ngx,)), dma((nb * ngx,)),
-            dma((1, ngy)), dma((1, ngy)),
             dma((nb * ngx * ngy,)), dma((nb * ngx * ngy,)),
         ],
         compiler_params=pltpu.CompilerParams(collective_id=0, has_side_effects=True,

time: 30.8 us -> 31 us (level)
  no operation moved by 1% of the time
where the time goes in v4:
time: 31 us; the launch traced here: 30.9 us
  Pallas kernels  28.9 us (93%)
  local copies, waits for them, and re-layouts  1.31 us (4%)
  between operations  0.64 us (2%)
    pallas_call x1, Pallas kernels, on_device(): pl.pallas_call(functools.partial(kernel, nb, ngx, ngy), out_shape=(pltpu....  28.9 us
    unnamed x2, local copies, waits for them, and re-layouts  1.31 us

profile of v4, /device:TPU:0, one launch (start us, length us, event | category | flops | bytes accessed | tf_op | source)
XLA Modules:
  0.0 30.9 jit_solution(3009253443933595333)
XLA Ops:
  0.6 28.9 %newton_step.1 = (f32[1,3,8,32,128]{4,3,2,1,0:T(8,128)S(1)}, f32[2,128]{1,0:T(2,128)S(1)}) custom-call(f32[1,3,8,32,128]{4,3,2,1,0:T(8,128)} %disp.1, f32[1,3,8,32,128]{4,3,2,1,0:T(8,128)} %force.1, f32[1,8,32,128]{3,2,1,0:T(8,128)} %kappa.1, f32[1,8,32,128]{3,2,1,0:T(8,128)} %sigma.1, f32[2,128]{1,0:T(2,128)} %gap0_in.1, f32[2,128]{1,0:T(2,128)} %press_in.1, ...), custom_call_target="tpu_custom_call" | custom-call | tf_op jit(solution)/shard_map/newton_step/pallas_call | solution.py:410
  29.6 0.7 %copy.13 = f32[1,3,8,32,128]{4,3,2,1,0:T(8,128)} copy(f32[1,3,8,32,128]{4,3,2,1,0:T(8,128)S(1)} %get-tuple-element.2) | data formatting | bytes 786432
  30.3 0.6 %copy.14 = f32[2,128]{1,0:T(2,128)} copy(f32[2,128]{1,0:T(2,128)S(1)} %get-tuple-element.3) | data formatting | bytes 2048

commit v5 on v4

--- a/solution.py
+++ b/solution.py
@@ -353,8 +353,10 @@
     vw = sum_of(v1_of, lambda c, x: v2[c, x]) + contact_sum(lambda l: cols[4, l], lambda l: cols[4, l])
 
     lane_of = lax.broadcasted_iota(jnp.int32, (1, sblk), 1)
+    packed = jnp.zeros((1, sblk), jnp.float32)
     for i, number in enumerate((rr, rv, vv, nn, nv, nw, vw, own)):
-        final[me, i : i + 1, :] = jnp.where(lane_of == lax.rem(me, sblk), number, 0.0)
+        packed = jnp.where(lane_of == i, number, packed)
+    final[me] = packed
     each_peer(lambda k: final_copy(k, False).start())
     for r, f in enumerate((f0, f1, f2)):
         halo_done(f, r)
@@ -367,16 +369,10 @@
                 u_copy(r, k, False).wait_send()
 
     each_peer(lambda k: final_copy(k, True).wait_recv())
-    groups = []
-    for start in range(0, count, sblk):
-        stop = min(start + sblk, count)
-        groups.append(lax.fori_loop(start + 1, stop, lambda w, t: t + final[w], final[start], unroll=count <= 64))
+    table = final[...].reshape(count, sblk)
 
     def over(act):
-        total = act(*[groups[0][i : i + 1, :] for i in range(8)])
-        for group in groups[1:]:
-            total = total + act(*[group[i : i + 1, :] for i in range(8)])
-        return jnp.sum(total, axis=1, keepdims=True)
+        return jnp.sum(act(*[table[:, i : i + 1] for i in range(8)]), axis=0, keepdims=True)
 
     norm0 = over(lambda rr, rv, vv, nn, nv, nw, vw, own: rr)
     alpha0 = norm0 / over(lambda rr, rv, vv, nn, nv, nw, vw, own: rv)
@@ -428,7 +424,7 @@
             pltpu.VMEM((3, nb, ngx, bpd, sblk), f32),
             pltpu.VMEM((2, ngx, bpd, sblk), f32),
             pltpu.VMEM((2, ngx, bpd, sblk), f32),
-            pltpu.VMEM((nb * ngx * ngy, 8, sblk), f32),
+            pltpu.VMEM((nb * ngx * ngy, 1, sblk), f32),
             pltpu.VMEM((6, bpd, sblk, 1), f32),
             dma((9,)),
             dma((3, len(DIRS))), dma((3, len(DIRS))),

time: 31 us -> 30.3 us (0.977)
  Pallas kernels: 28.9 us -> 28.2 us
    pallas_call x1, Pallas kernels: 28.9 us -> 28.2 us  [on_device(): pl.pallas_call(functools.partial(kernel, nb, ngx, ngy), out_shape=(pltpu....]
where the time goes in v5:
time: 30.3 us; the launch traced here: 30.2 us
  Pallas kernels  28.2 us (93%)
  local copies, waits for them, and re-layouts  1.31 us (4%)
  between operations  0.64 us (2%)
    pallas_call x1, Pallas kernels, on_device(): pl.pallas_call(functools.partial(kernel, nb, ngx, ngy), out_shape=(pltpu....  28.2 us
    unnamed x2, local copies, waits for them, and re-layouts  1.31 us

profile of v5, /device:TPU:0, one launch (start us, length us, event | category | flops | bytes accessed | tf_op | source)
XLA Modules:
  0.0 30.2 jit_solution(3672864587801687180)
XLA Ops:
  0.6 28.2 %newton_step.1 = (f32[1,3,8,32,128]{4,3,2,1,0:T(8,128)S(1)}, f32[2,128]{1,0:T(2,128)S(1)}) custom-call(f32[1,3,8,32,128]{4,3,2,1,0:T(8,128)} %disp.1, f32[1,3,8,32,128]{4,3,2,1,0:T(8,128)} %force.1, f32[1,8,32,128]{3,2,1,0:T(8,128)} %kappa.1, f32[1,8,32,128]{3,2,1,0:T(8,128)} %sigma.1, f32[2,128]{1,0:T(2,128)} %gap0_in.1, f32[2,128]{1,0:T(2,128)} %press_in.1, ...), custom_call_target="tpu_custom_call" | custom-call | tf_op jit(solution)/shard_map/newton_step/pallas_call | solution.py:406
  28.9 0.7 %copy.13 = f32[1,3,8,32,128]{4,3,2,1,0:T(8,128)} copy(f32[1,3,8,32,128]{4,3,2,1,0:T(8,128)S(1)} %get-tuple-element.2) | data formatting | bytes 786432
  29.6 0.6 %copy.14 = f32[2,128]{1,0:T(2,128)} copy(f32[2,128]{1,0:T(2,128)S(1)} %get-tuple-element.3) | data formatting | bytes 2048
